TPU v7x, 32 devices: a whole 2x2x4 slice. The times are simulated.
32 devices in a mesh: fsdp: 8 (over y, x, core), tp: 4 (over z).
Axes of the slice: x: 2, y: 2, z: 4, core: 2. Of those that a mesh axis runs over, the one named last changes fastest.
Arguments:
- tokens: bfloat16 [14336, 768], P(('fsdp', 'tp')), may hold values from -6 to 6
- cotangent: bfloat16 [14336, 768], P(('fsdp', 'tp')), may hold values from -6 to 6
- block_segment: int32 [112], P('fsdp'), may hold values from 0 to 6, as said below
- segment_path: int32 [56, 7], P('fsdp'), may hold values from 0 to 1, as said below
- norm1_gain: bfloat16 [768], P('fsdp'), may hold values from 0.5 to 1.5
- norm1_bias: bfloat16 [768], P('fsdp'), may hold values from -1.796875 to 1.796875
- norm2_gain: bfloat16 [768], P('fsdp'), may hold values from 0.5 to 1.5
- norm2_bias: bfloat16 [768], P('fsdp'), may hold values from -1.796875 to 1.796875
- query_weight: bfloat16 [768, 768], P('fsdp', 'tp'), may hold values from -0.21875 to 0.21875
- query_bias: bfloat16 [4, 192], P('tp', 'fsdp'), may hold values from -1.796875 to 1.796875
- kv_weight: bfloat16 [768, 128], P('fsdp'), may hold values from -0.21875 to 0.21875
- kv_bias: bfloat16 [128], P('fsdp'), may hold values from -1.796875 to 1.796875
- out_weight: bfloat16 [768, 768], P('tp', 'fsdp'), may hold values from -3.5 to 3.5
- out_bias: bfloat16 [768], P('fsdp'), may hold values from -1.796875 to 1.796875
- up_weight: bfloat16 [768, 3072], P('fsdp', 'tp'), may hold values from -0.21875 to 0.21875
- up_bias: bfloat16 [4, 768], P('tp', 'fsdp'), may hold values from -1.796875 to 1.796875
- down_weight: bfloat16 [3072, 768], P('tp', 'fsdp'), may hold values from -0.109375 to 0.109375
- down_bias: bfloat16 [768], P('fsdp'), may hold values from -1.796875 to 1.796875
Outputs:
- output: bfloat16 [14336, 768], P(('fsdp', 'tp'))
- keys_values: bfloat16 [14336, 128], P(('fsdp', 'tp'))
- input_grad: bfloat16 [14336, 768], P(('fsdp', 'tp'))
- grad_norm1_gain: float32 [768], P('fsdp')
- grad_norm1_bias: float32 [768], P('fsdp')
- grad_norm2_gain: float32 [768], P('fsdp')
- grad_norm2_bias: float32 [768], P('fsdp')
- grad_query_weight: float32 [768, 768], P('fsdp', 'tp')
- grad_query_bias: float32 [4, 192], P('tp', 'fsdp')
- grad_kv_weight: float32 [768, 128], P('fsdp')
- grad_kv_bias: float32 [128], P('fsdp')
- grad_out_weight: float32 [768, 768], P('tp', 'fsdp')
- grad_out_bias: float32 [768], P('fsdp')
- grad_up_weight: float32 [768, 3072], P('fsdp', 'tp')
- grad_up_bias: float32 [4, 768], P('tp', 'fsdp')
- grad_down_weight: float32 [3072, 768], P('tp', 'fsdp')
- grad_down_bias: float32 [768], P('fsdp')
Inputs may be any that keep to these rules, and one draw needn't show every extreme that they name: `block_segment`: the 14 blocks of one index of fsdp hold one tree. A tree's 14 blocks are its trunk (8 blocks of one segment), then its 2 branches and then its 4 leaves, one block each. Tree t of its index numbers its 7 segments t * 7 to t * 7 + 6, each once, in an order drawn from the seed. `segment_path`: rows g * 7 to g * 7 + 6 are the table of index g of fsdp: entry [s, t] is 1 where segment t is s itself, the trunk of s's tree, or, for a leaf s, the branch that it grows from (each branch has exactly 2 leaves), and 0 otherwise.
All inputs are finite; a program needn't handle non-finite values.
Results may differ from a plain program's by a relative error of at most 0.013.
Values may be sent and summed in bfloat16 or wider, within the bound.
No kernel may reach another device: no remote copies, remote signals or barrier semaphores. Data moves between devices by JAX's collectives and lax.ppermute only.
A program may use at most 192 MiB of HBM per device.

v0:
```python
import math

import jax
import jax.numpy as jnp
from jax import lax
from jax.experimental import pallas as pl
from jax.experimental.pallas import tpu as pltpu
from jax.sharding import PartitionSpec as P


HD = 64
ROT = 16
BLK = 128
TRUNK = 8
FIRST_LEAF = 10
TILE = 64
HEADS_STEP = 4
NORM_EPS = 1e-05
MASKED = -1000000000.0
BF = jnp.bfloat16
F32 = jnp.float32


def dot(left, right, left_dim, right_dim):
    return lax.dot_general(
        left, right, (((left_dim,), (right_dim,)), ((), ())), preferred_element_type=F32
    )


def add_low(left, right):
    return (left.astype(F32) + right.astype(F32)).astype(BF)


def swap(value, axis, bit):
    count = lax.axis_size(axis)
    return lax.ppermute(value, axis, [(i, i ^ bit) for i in range(count)])


def swap_fsdp(value, bit):
    return swap(value, "fsdp", bit)


def swap_tp(value, bit):
    return swap(value, "tp", bit)


def bits_of(count):
    return [1 << k for k in range(count.bit_length() - 1)]


def core_order(mine, other, axis=0):
    core = lax.axis_index("fsdp") & 1
    return jnp.where(
        core == 0,
        jnp.concatenate([mine, other], axis=axis),
        jnp.concatenate([other, mine], axis=axis),
    )


def direct(count):
    return count == 8


def chip_gather(value):
    count = lax.axis_size("fsdp")
    if direct(count):
        return [value] + [swap_fsdp(value, bit) for bit in (2, 4, 6)]
    for bit in bits_of(count)[1:]:
        value = jnp.concatenate([value, swap_fsdp(value, bit)], axis=0)
    return [relative(value, 0, "fsdp")]


def chip_scatter(kept, sent, bits):
    value = kept
    if sent is None:
        value = relative(kept.reshape(-1, kept.shape[2]), 0, "fsdp")
        bits = bits_of(lax.axis_size("fsdp"))[:0:-1]
        value = value.reshape(bits[0], -1, kept.shape[2])
    else:
        value = add_low(kept, swap_fsdp(sent, bits[0]))
        bits = bits[1:]
    for bit in bits:
        half = value.shape[0] // 2
        value = add_low(value[:half], swap_fsdp(value[half:], bit))
    return value[0]


def tp_gather(value, axis):
    count = lax.axis_size("tp")
    pieces = {0: value}
    for bit in reversed(bits_of(count)):
        order = sorted(pieces)
        sent = [pieces[r] for r in order]
        taken = swap_tp(sent[0] if len(sent) == 1 else jnp.concatenate(sent, axis=axis), bit)
        size = taken.shape[axis] // len(order)
        for place, r in enumerate(order):
            pieces[r | bit] = lax.slice_in_dim(taken, place * size, (place + 1) * size, axis=axis)
    return [pieces[r] for r in range(count)]


def tp_scatter(pieces, axis):
    pieces = dict(enumerate(pieces))
    bits = bits_of(len(pieces))
    for bit in bits:
        kept = [r for r in sorted(pieces) if not r & bit]
        sent = [pieces[r | bit] for r in kept]
        sent = sent[0] if len(sent) == 1 else jnp.concatenate(sent, axis=axis)
        taken = swap_tp(sent.astype(BF), bit).astype(F32)
        size = taken.shape[axis] // len(kept)
        pieces = {
            r: pieces[r].astype(F32)
            + lax.slice_in_dim(taken, place * size, (place + 1) * size, axis=axis)
            for place, r in enumerate(kept)
        }
    return pieces[0]


def tp_scatter_even(value, size):
    count = value.shape[1] // size // 2
    blocks = [value[:, k * size : (k + 1) * size] for k in range(2 * count)]
    ups, downs = blocks[:count], blocks[count:]
    for bit in reversed(bits_of(lax.axis_size("tp"))[1:]):
        count //= 2
        taken = swap_tp(jnp.concatenate(ups[count:] + downs[count:], axis=1), bit)
        taken = [taken[:, k * size : (k + 1) * size].astype(F32) for k in range(2 * count)]
        ups = [ups[k].astype(F32) + taken[k] for k in range(count)]
        downs = [downs[k].astype(F32) + taken[count + k] for k in range(count)]
    return jnp.concatenate(ups + downs, axis=1)


def relative(value, axis, name):
    count = lax.axis_size(name)
    index = lax.axis_index(name)
    if name == "fsdp":
        count, index = count // 2, index // 2
    size = value.shape[axis] // count
    blocks = [lax.slice_in_dim(value, k * size, (k + 1) * size, axis=axis) for k in range(count)]
    for bit in bits_of(count):
        taken = (index & bit) != 0
        blocks = [jnp.where(taken, blocks[k ^ bit], blocks[k]) for k in range(count)]
    return jnp.concatenate(blocks, axis=axis)


def attention_kernel(first, *refs):
    (
        meta_ref,
        query_ref,
        grad_ref,
        kv_ref,
        cos_ref,
        back_ref,
        ahead_ref,
    ) = refs[:7]
    refs = refs[7:]
    earlier = None
    if first:
        earlier = refs[2]
        refs = refs[3:]
    (
        attended_ref,
        query_grad_ref,
        kv_grad_ref,
        queries,
        grads,
        outs,
        query_grads,
        keys,
        values,
        key_acc,
        value_acc,
        bias,
    ) = refs
    step = pl.program_id(0)
    pair_count = query_ref.shape[1] // 128
    groups = queries.shape[0]
    trunk = TRUNK * BLK
    block = meta_ref[step + first, 0]
    offset = meta_ref[step + first, 1]
    parent = meta_ref[step + first, 2]

    @pl.when(step == 0)
    def _():
        if earlier is None:
            kv_grad_ref[...] = jnp.zeros_like(kv_grad_ref)
        else:
            kv_grad_ref[...] = earlier[...]
        keys[:trunk, :] = kv_ref[:trunk, :HD]
        values[:trunk, :] = kv_ref[:trunk, HD:]

    parent_rows = pl.ds(pl.multiple_of(parent * BLK, BLK), BLK)
    own_rows = pl.ds(pl.multiple_of(block * BLK, BLK), BLK)
    keys[trunk : trunk + BLK, :] = kv_ref[parent_rows, :HD]
    values[trunk : trunk + BLK, :] = kv_ref[parent_rows, HD:]
    keys[trunk + BLK :, :] = kv_ref[own_rows, :HD]
    values[trunk + BLK :, :] = kv_ref[own_rows, HD:]

    row = lax.broadcasted_iota(jnp.int32, bias.shape, 0) + offset
    col = lax.broadcasted_iota(jnp.int32, bias.shape, 1)
    in_trunk = block < TRUNK
    trunk_limit = jnp.where(in_trunk, block * BLK + row, trunk)
    own_limit = jnp.where(in_trunk, -1, row)
    is_leaf = (block >= FIRST_LEAF).astype(jnp.int32)
    parent_limit = is_leaf * (2 * trunk) - 1
    limit = jnp.where(
        col < trunk, trunk_limit, jnp.where(col < trunk + BLK, parent_limit, own_limit + trunk + BLK)
    )
    bias[...] = jnp.where(col <= limit, 0.0, MASKED)

    cos = cos_ref[...]
    back = back_ref[...]
    ahead = ahead_ref[...]
    per_group = HEADS_STEP // 2
    for pair in range(pair_count):
        lanes = slice(pair * 128, (pair + 1) * 128)
        linear = query_ref[:, lanes]
        turned = (
            linear * cos
            + pltpu.roll(linear, 128 - ROT // 2, 1) * back
            + pltpu.roll(linear, ROT // 2, 1) * ahead
        ).astype(BF) * jnp.asarray(1.0 / math.sqrt(HD), BF)
        grad = grad_ref[:, lanes]
        group, place = divmod(pair, per_group)
        for side in range(2):
            rows = slice((2 * place + side) * TILE, (2 * place + side + 1) * TILE)
            queries[group, rows, :] = turned[:, side * HD : (side + 1) * HD]
            grads[group, rows, :] = grad[:, side * HD : (side + 1) * HD]

    key_acc[...] = jnp.zeros_like(key_acc)
    value_acc[...] = jnp.zeros_like(value_acc)

    def one_group(group, carry):
        query = queries[group]
        grad = grads[group]
        key = keys[...]
        value = values[...]
        score = dot(query, key, 1, 1)
        score = (score.reshape(HEADS_STEP, TILE, -1) + bias[...][None]).reshape(score.shape)
        peak = jnp.max(score, axis=1, keepdims=True)
        exponent = jnp.exp(score - peak)
        total = jnp.sum(exponent, axis=1, keepdims=True)
        prob = exponent * (1.0 / total)
        prob_low = prob.astype(BF)
        outs[group] = dot(prob_low, value, 1, 0)
        grad_prob = dot(grad, value, 1, 1)
        delta = jnp.sum(prob * grad_prob, axis=1, keepdims=True)
        score_grad = (prob * (grad_prob - delta)).astype(BF)
        query_grads[group] = dot(score_grad, key, 1, 0)
        key_acc[...] += dot(score_grad, query, 0, 0)
        value_acc[...] += dot(prob_low, grad, 0, 0)
        return carry

    lax.fori_loop(0, groups, one_group, 0)

    scale = 1.0 / math.sqrt(HD)
    for pair in range(pair_count):
        lanes = slice(pair * 128, (pair + 1) * 128)
        group, place = divmod(pair, per_group)
        first = slice(2 * place * TILE, (2 * place + 1) * TILE)
        second = slice((2 * place + 1) * TILE, (2 * place + 2) * TILE)
        attended_ref[:, lanes] = jnp.concatenate(
            [outs[group, first, :], outs[group, second, :]], axis=1
        ).astype(BF)
        turned = scale * jnp.concatenate(
            [query_grads[group, first, :], query_grads[group, second, :]], axis=1
        )
        query_grad_ref[:, lanes] = (
            turned * cos
            - pltpu.roll(turned, 128 - ROT // 2, 1) * back
            - pltpu.roll(turned, ROT // 2, 1) * ahead
        ).astype(BF)
    kv_grad_ref[:trunk, :HD] += key_acc[:trunk, :]
    kv_grad_ref[:trunk, HD:] += value_acc[:trunk, :]
    kv_grad_ref[parent_rows, :HD] += key_acc[trunk : trunk + BLK, :]
    kv_grad_ref[parent_rows, HD:] += value_acc[trunk : trunk + BLK, :]
    kv_grad_ref[own_rows, :HD] += key_acc[trunk + BLK :, :]
    kv_grad_ref[own_rows, HD:] += value_acc[trunk + BLK :, :]


def attention(meta, query_lin, grad_attended, key_value, cos, back, ahead, first, last, earlier):
    rows, width = query_lin.shape
    groups = width // HD // HEADS_STEP
    seen = (TRUNK + 2) * BLK
    stacked = HEADS_STEP * TILE
    tile = lambda lanes: pl.BlockSpec((TILE, lanes), lambda i, m: (i + first, 0))
    whole = pl.BlockSpec(key_value.shape, lambda i, m: (0, 0))
    anywhere = pl.BlockSpec(memory_space=pl.ANY)
    given = [] if earlier is None else [anywhere, anywhere, whole]
    count = last - first
    work = 6 * count * TILE * (width // HD) * seen
    return pl.pallas_call(
        lambda *refs: attention_kernel(first, *refs),
        out_shape=(
            jax.ShapeDtypeStruct((rows, width), BF),
            jax.ShapeDtypeStruct((rows, width), BF),
            jax.ShapeDtypeStruct(key_value.shape, F32),
        ),
        grid_spec=pltpu.PrefetchScalarGridSpec(
            num_scalar_prefetch=1,
            grid=(count,),
            in_specs=[tile(width), tile(width), whole, tile(128), tile(128), tile(128)] + given,
            out_specs=[tile(width), tile(width), whole],
            scratch_shapes=[
                pltpu.VMEM((groups, stacked, HD), BF),
                pltpu.VMEM((groups, stacked, HD), BF),
                pltpu.VMEM((groups, stacked, HD), F32),
                pltpu.VMEM((groups, stacked, HD), F32),
                pltpu.VMEM((seen, HD), BF),
                pltpu.VMEM((seen, HD), BF),
                pltpu.VMEM((seen, HD), F32),
                pltpu.VMEM((seen, HD), F32),
                pltpu.VMEM((TILE, seen), F32),
            ],
        ),
        input_output_aliases={} if earlier is None else {7: 0, 8: 1},
        cost_estimate=pl.CostEstimate(
            flops=2 * 256 * work, bytes_accessed=2 * rows * width, transcendentals=work // 6
        ),
        compiler_params=pltpu.CompilerParams(vmem_limit_bytes=40 * 2**20),
    )(meta, query_lin, grad_attended, key_value, cos, back, ahead, *(earlier or ()))


def local_kernel(kernel, outs, args, scratch=(), flops=0, scalars=1):
    return pl.pallas_call(
        kernel,
        out_shape=[jax.ShapeDtypeStruct(shape, kind) for shape, kind in outs],
        in_specs=[pl.BlockSpec(memory_space=pltpu.SMEM)] * scalars
        + [pl.BlockSpec(memory_space=pltpu.VMEM)] * (len(args) - scalars),
        out_specs=[pl.BlockSpec(memory_space=pltpu.VMEM)] * len(outs),
        scratch_shapes=list(scratch),
        cost_estimate=pl.CostEstimate(flops=flops, bytes_accessed=2**20, transcendentals=0),
        compiler_params=pltpu.CompilerParams(vmem_limit_bytes=56 * 2**20),
    )(*args)


def identity(size):
    row = lax.broadcasted_iota(jnp.int32, (size, size), 0)
    col = lax.broadcasted_iota(jnp.int32, (size, size), 1)
    return jnp.where(row == col, 1.0, 0.0).astype(BF)


LINES = 16


def pack_kernel(place, query, out, up, down, kv, *refs):
    lines = refs[:-4]
    kept, sent, small, buffer = refs[-4:]
    core = place[0]
    shard, heads = query.shape
    half = up.shape[1] // 2
    unit = identity(shard)
    out_turned = dot(unit, out[...], 1, 1).astype(BF)
    down_turned = dot(unit, down[...], 1, 1).astype(BF)
    first = core == 0

    def pair(one, two, at):
        size = one.shape[1]
        one, two = one.astype(F32), two.astype(F32)
        kept[:, at : at + size] = jnp.where(first, one, two).astype(BF)
        sent[:, at : at + size] = jnp.where(first, two, one).astype(BF)

    pair(query[...], out_turned, 0)
    pair(up[:, :half], up[:, half:], heads)
    pair(down_turned[:, :half], down_turned[:, half:], heads + half)
    buffer[...] = jnp.zeros_like(buffer)
    for k, line in enumerate(lines):
        buffer[k : k + 1, : line.shape[1]] = line[...].astype(F32)
    small[:LINES, :] = buffer[...].astype(BF)
    small[LINES:, :] = kv[...]


def block_at(chip, k, size):
    return pl.ds(pl.multiple_of((chip ^ k) * size, size), size)


def place_kernel(place, *refs):
    out = refs[-1]
    for k, ref in enumerate(refs[:-1]):
        out[block_at(place[1], k, ref.shape[0]), :] = ref[...]


def send_order(bits):
    order = [0]
    for bit in reversed(bits):
        order = order + [k | bit for k in order]
    return order


def put_blocks(chip, source, kept, sent, bits):
    count = kept.shape[0] + (sent.shape[0] if sent is not None else 0)
    size = kept.shape[1]
    order = send_order(bits) if sent is not None else [0]
    for spot, k in enumerate(order):
        rows = block_at(chip, k, size) if count > 1 else slice(None)
        value = source[rows, :].astype(BF)
        if spot < kept.shape[0]:
            kept[spot] = value
        else:
            sent[spot - kept.shape[0]] = value


def mat_grad_kernel(place, one, query_low, grad, attended, kept, sent, first, second):
    core = place[0]
    first[...] = dot(one[...], query_low[...], 0, 0)
    second[...] = dot(grad[...], attended[...], 0, 0)
    count, size = kept.shape[:2]
    for k in range(count):
        rows = block_at(place[1], k, size) if count > 1 else slice(None)
        here, there = first[rows, :], second[rows, :]
        kept[k] = jnp.where(core == 0, here, there).astype(BF)
        sent[k] = jnp.where(core == 0, there, here).astype(BF)


def ffn_kernel(weight_count, sending, *refs):
    place, gain, shift, up_shift = refs[:4]
    token_refs, grad_refs = refs[4:8], refs[8:12]
    weights = refs[12 : 12 + weight_count]
    refs = refs[12 + weight_count :]
    kept, sent, sums = refs[:3]
    up_kept, down_kept = refs[3:5]
    up_sent, down_sent = refs[5:7] if sending else (None, None)
    tokens, grads, up, down, two_all, low_all, act_all, total = refs[7 if sending else 5 :]
    hidden_own = up.shape[1]
    tile = tokens.shape[1]
    pieces = tokens.shape[0]
    for k in range(4):
        for side in range(2):
            tokens[2 * k + side] = token_refs[k][side * tile : (side + 1) * tile, :]
            grads[2 * k + side] = grad_refs[k][side * tile : (side + 1) * tile, :]
    for k, ref in enumerate(weights):
        rows = block_at(place[1], k, ref.shape[0]) if weight_count > 1 else slice(None)
        up[rows, :] = ref[:, :hidden_own]
        down[rows, :] = ref[:, hidden_own:]
    sums[...] = jnp.zeros_like(sums)

    def one_tile(i, carry):
        value = tokens[i].astype(F32)
        centred = value - jnp.mean(value, axis=1, keepdims=True)
        variance = jnp.mean(centred * centred, axis=1, keepdims=True)
        normal = centred * lax.rsqrt(variance + NORM_EPS)
        two = (normal * gain[...] + shift[...]).astype(BF)
        hidden = dot(two, up[...], 1, 0) + up_shift[...]
        below = 0.5 * (1.0 + lax.erf(hidden * (1.0 / math.sqrt(2.0))))
        active = (hidden * below).astype(BF)
        bell = jnp.exp(-0.5 * hidden * hidden) * (1.0 / math.sqrt(2.0 * math.pi))
        grad = grads[i]
        slope_grad = dot(grad, down[...], 1, 0) * (below + hidden * bell)
        low = slope_grad.astype(BF)
        branch = dot(active, down[...], 1, 1)
        norm_grad = dot(low, up[...], 1, 1)
        rows = pl.ds(pl.multiple_of(i * tile, tile), tile)
        two_all[rows, :] = two
        low_all[rows, :] = low
        act_all[rows, :] = active
        sums[0:1, :] += jnp.sum(norm_grad * normal, axis=0, keepdims=True)
        sums[1:2, :] += jnp.sum(norm_grad, axis=0, keepdims=True)
        sums[2:3, :hidden_own] += jnp.sum(low.astype(F32), axis=0, keepdims=True)
        branch = branch.astype(BF)
        norm_grad = norm_grad.astype(BF)

        @pl.when(i < pieces // 2)
        def _():
            kept[0, i] = branch
            kept[1, i] = norm_grad

        @pl.when(i >= pieces // 2)
        def _():
            sent[0, i - pieces // 2] = branch
            sent[1, i - pieces // 2] = norm_grad

        return carry

    lax.fori_loop(0, pieces, one_tile, 0)
    total[...] = dot(two_all[...], low_all[...], 0, 0)
    put_blocks(place[1], total, up_kept, up_sent, (1, 2))
    flat = grads[...].reshape(act_all.shape[0], -1)
    total[...] = dot(flat, act_all[...], 0, 0)
    put_blocks(place[1], total, down_kept, down_sent, (2, 1))


def tree_tables(block_segment, segment_path, rank, rows):
    blocks = block_segment.shape[0]
    seg_count = segment_path.shape[1]
    one_hot = (block_segment[:, None] == jnp.arange(seg_count)[None, :]).astype(F32)
    linked = jnp.dot(jnp.dot(one_hot, segment_path.astype(F32)), one_hot.T)
    order = jnp.arange(blocks)
    before = jnp.sum(jnp.where(order[:, None] > order[None, :], linked, 0.0), axis=1)
    first_row = rank * rows
    row = first_row + jnp.arange(rows, dtype=jnp.int32)
    own = (row[:, None] // BLK == order[None, :]).astype(F32)
    position = jnp.sum(own * before[None, :], axis=1) * BLK + (row % BLK).astype(F32)
    start = first_row + TILE * jnp.arange(rows // TILE, dtype=jnp.int32)
    block = start // BLK
    second = jnp.sum((block[:, None] == order[None, :]) * linked[None, :, TRUNK + 1], axis=1)
    parent = jnp.where((block >= FIRST_LEAF) & (second > 0.5), TRUNK + 1, TRUNK)
    meta = jnp.stack([block, start % BLK, parent], axis=1).astype(jnp.int32)
    return position, meta


def body(
    tokens,
    cotangent,
    block_segment,
    segment_path,
    norm1_gain,
    norm1_bias,
    norm2_gain,
    norm2_bias,
    query_weight,
    query_bias,
    kv_weight,
    kv_bias,
    out_weight,
    out_bias,
    up_weight,
    up_bias,
    down_weight,
    down_bias,
):
    fsdp_count = lax.axis_size("fsdp")
    tp_count = lax.axis_size("tp")
    chips = fsdp_count // 2
    core = lax.axis_index("fsdp") & 1
    rank = lax.axis_index("tp")
    rows, width = tokens.shape
    shard = norm1_gain.shape[0]
    hidden_half = up_weight.shape[1] // 2
    heads_tp = query_weight.shape[1]
    chip = lax.axis_index("fsdp") // 2
    blocks = chips if direct(fsdp_count) else 1
    place = jnp.stack([core, chip]).astype(jnp.int32)
    pick = lambda first, second: jnp.where(core == 0, first, second)

    lines = [norm1_gain, norm1_bias, norm2_gain, norm2_bias, out_bias, down_bias, kv_bias]
    lines = [line[None, :] for line in lines] + [query_bias, up_bias]
    packed = heads_tp + 2 * hidden_half
    kept, sent, small = local_kernel(
        pack_kernel,
        [((shard, packed), BF), ((shard, packed), BF), ((LINES + shard, 128), BF)],
        [place, query_weight, out_weight, up_weight, down_weight, kv_weight, *lines],
        [pltpu.VMEM((LINES, 128), F32)],
    )
    small = small[None]
    small = core_order(small, swap_fsdp(small, 1))
    piece = core_order(kept, swap_fsdp(sent, 1))
    grad_core = swap_fsdp(cotangent, 1)
    tokens_core = swap_fsdp(tokens, 1)
    mat_piece = jnp.concatenate(tp_gather(piece[:, :heads_tp], 1), axis=1)
    mat_pieces = chip_gather(mat_piece)
    if blocks > 1:
        mat_kept = local_kernel(place_kernel, [((width, width), BF)], [place, *mat_pieces])[0]
    else:
        mat_kept = mat_pieces[0]
    mat_other = swap_fsdp(mat_kept, 1)
    query_mat = pick(mat_kept, mat_other)
    out_mat = pick(mat_other, mat_kept)

    for bit in bits_of(fsdp_count)[1:]:
        small = jnp.concatenate([small, swap_fsdp(small, bit)], axis=0)
    small = relative(small.reshape(chips, -1), 0, "fsdp").reshape(small.shape)
    kv_mat = small[:, LINES:].reshape(width, -1)
    line_at = lambda k, size: small[:, k, :size].reshape(1, -1)
    gain_one, shift_one, gain_two, shift_two, out_shift, down_shift = (
        line_at(k, shard).astype(F32) for k in range(6)
    )
    kv_shift = line_at(6, kv_bias.shape[0]).astype(F32)
    query_own = line_at(7, query_bias.shape[1])
    up_own = line_at(8, up_bias.shape[1])
    up_own = pick(up_own[:, :hidden_half], up_own[:, hidden_half:])
    shifts = jnp.concatenate(tp_gather(jnp.concatenate([query_own, up_own], axis=1), 0), axis=0)
    shifts = shifts.astype(F32)
    query_shift = shifts[:, :heads_tp].reshape(-1)
    up_shift = shifts[::2, heads_tp:].reshape(1, -1)

    inputs = tokens.astype(F32)
    centred = inputs - jnp.mean(inputs, axis=-1, keepdims=True)
    inverse = lax.rsqrt(jnp.mean(centred * centred, axis=-1, keepdims=True) + NORM_EPS)
    normal = centred * inverse
    low_one = (normal * gain_one + shift_one).astype(BF)

    ffn_piece, tokens_sent, grad_sent, _ = lax.optimization_barrier(
        (piece[:, heads_tp:], tokens, cotangent, mat_piece)
    )
    ups = [ffn_piece[:, :hidden_half]]
    downs = [ffn_piece[:, hidden_half:]]
    for bit in bits_of(tp_count)[1:]:
        near = swap_tp(jnp.concatenate(ups + downs, axis=1), bit)
        near = [near[:, k * hidden_half : (k + 1) * hidden_half] for k in range(2 * len(ups))]
        ups, downs = ups + near[: len(ups)], downs + near[len(ups) :]
    ffn_piece = jnp.concatenate(ups + downs, axis=1)
    ffn_piece, mat_pieces[-1] = lax.optimization_barrier((ffn_piece, mat_pieces[-1]))
    ffn_pieces = chip_gather(ffn_piece)
    hidden_own = hidden_half * tp_count // 2
    tokens_tp = swap_tp(tokens_sent, 1)
    grad_tp = swap_tp(grad_sent, 1)

    position, meta = tree_tables(block_segment, segment_path, rank, rows)
    lane = jnp.arange(128, dtype=jnp.int32)
    frequency = jnp.exp((lane % (ROT // 2)).astype(F32) * (-2.0 * math.log(10000.0) / ROT))
    phase = position[:, None] * frequency[None, :]
    cos_wave = jnp.cos(phase)
    sin_wave = jnp.sin(phase)
    in_head = lane % HD
    cos = jnp.where(in_head < ROT, cos_wave, 1.0)
    back = jnp.where(in_head < ROT // 2, -sin_wave, 0.0)
    ahead = jnp.where((in_head >= ROT // 2) & (in_head < ROT), sin_wave, 0.0)
    is_key = lane < HD
    cos_key = jnp.where(is_key, cos, 1.0)
    back_key = jnp.where(is_key, back, 0.0)
    ahead_key = jnp.where(is_key, ahead, 0.0)

    kv_lin = dot(low_one, kv_mat, 1, 0) + kv_shift
    key_cache = (
        kv_lin * cos_key
        + jnp.roll(kv_lin, -(ROT // 2), 1) * back_key
        + jnp.roll(kv_lin, ROT // 2, 1) * ahead_key
    ).astype(BF)
    kv_all = relative(jnp.concatenate(tp_gather(key_cache, 0), axis=0), 0, "tp")

    query_lin = dot(low_one, query_mat, 1, 0) + query_shift
    grad_attended = dot(cotangent, out_mat, 1, 0).astype(BF)
    tiles = rows // TILE
    middle = tiles * 5 // 7
    operands = (meta, query_lin, grad_attended, kv_all, cos, back, ahead)
    earlier = attention(*operands, 0, middle, None)
    tokens_tp, grad_tp, *earlier = lax.optimization_barrier((tokens_tp, grad_tp, *earlier))
    tokens_far = swap_fsdp(tokens_tp, 1)
    grad_far = swap_fsdp(grad_tp, 1)
    attended, query_low, kv_grad = attention(*operands, middle, tiles, tuple(earlier))

    first_token, attended, query_low, kv_grad = lax.optimization_barrier(
        (tokens, attended, query_low, kv_grad)
    )
    half = rows // 2
    block_rows = width // blocks
    halves = [((2, 4, half, width), BF)] * 2 + [((8, max(width, hidden_own)), F32)]
    grad_kept = [((max(blocks // 2, 1), block_rows, hidden_own), BF)] * 2
    grad_sent = grad_kept if blocks > 1 else []
    ffn_out = local_kernel(
        lambda *refs: ffn_kernel(len(ffn_pieces), blocks > 1, *refs),
        halves + grad_kept + grad_sent,
        [
            *(place, gain_two, shift_two, up_shift),
            *(first_token, tokens_tp, tokens_core, tokens_far),
            *(cotangent, grad_tp, grad_core, grad_far),
            *ffn_pieces,
        ],
        [
            pltpu.VMEM((8, half, width), BF),
            pltpu.VMEM((8, half, width), BF),
            pltpu.VMEM((width, hidden_own), BF),
            pltpu.VMEM((width, hidden_own), BF),
            pltpu.VMEM((4 * rows, width), BF),
            pltpu.VMEM((4 * rows, hidden_own), BF),
            pltpu.VMEM((4 * rows, hidden_own), BF),
            pltpu.VMEM((width, hidden_own), F32),
        ],
        flops=12 * 4 * rows * width * hidden_own,
    )
    part_kept, part_sent, ffn_vectors, up_kept, down_kept = ffn_out[:5]
    up_sent, down_sent = ffn_out[5:] if blocks > 1 else (None, None)
    part = part_kept.astype(F32) + swap_fsdp(part_sent, 1).astype(F32)
    part_tp = swap_tp(part[:, 2:].astype(BF), 1)
    up_sum = chip_scatter(up_kept, up_sent, (2, 4))
    down_sum = chip_scatter(down_kept, down_sent, (4, 2))
    ffn_sum = tp_scatter_even(jnp.concatenate([up_sum, down_sum], axis=1), hidden_half)
    ffn_own = pick(ffn_sum[:shard], ffn_sum[shard:])
    ffn_other = swap_fsdp(pick(ffn_sum[shard:], ffn_sum[:shard]), 1)
    up_mat_sum = core_order(ffn_own[:, :hidden_half], ffn_other[:, :hidden_half], axis=1)
    down_mat_sum = core_order(ffn_own[:, hidden_half:], ffn_other[:, hidden_half:], axis=1).T
    up_shift_grad = ffn_vectors[2, :hidden_own].reshape(-1, hidden_half)

    attended_out = dot(attended, out_mat, 1, 1)
    kv_pieces = relative(kv_grad, 0, "tp").reshape(tp_count, rows, -1)
    kv_sum = tp_scatter([kv_pieces[r] for r in range(tp_count)], 0)
    kv_low_grad = (
        kv_sum * cos_key
        - jnp.roll(kv_sum, -(ROT // 2), 1) * back_key
        - jnp.roll(kv_sum, ROT // 2, 1) * ahead_key
    ).astype(BF)
    mat_own, mat_given = local_kernel(
        mat_grad_kernel,
        [((blocks, block_rows, width), BF)] * 2,
        [place, low_one, query_low, cotangent, attended],
        [pltpu.VMEM((width, width), F32)] * 2,
        flops=4 * rows * width * width,
    )
    grad_kv_mat = dot(low_one, kv_low_grad, 0, 0)
    norm_one_grad = dot(query_low, query_mat, 1, 1) + dot(kv_low_grad, kv_mat, 1, 1)
    mat_own = add_low(mat_own, swap_fsdp(mat_given, 1))
    if blocks > 1:
        side = width // 2
        left = chip_scatter(mat_own[::2, :, :side], mat_own[1::2, :, :side], (2, 4))
        right = chip_scatter(mat_own[:2, :, side:], mat_own[2:, :, side:], (4, 2))
        mat_sum = jnp.concatenate([left, right], axis=1)
    else:
        mat_sum = chip_scatter(mat_own, None, None)
    mat_sum = tp_scatter(
        [mat_sum[:, r * heads_tp : (r + 1) * heads_tp] for r in range(tp_count)], 1
    )
    mat_own = pick(mat_sum[:shard], mat_sum[shard:])
    mat_away = swap_fsdp(pick(mat_sum[shard:], mat_sum[:shard]), 1)
    query_mat_sum = pick(mat_own, mat_away)
    out_mat_sum = pick(mat_away, mat_own).T

    features = jnp.stack(
        [
            jnp.sum(norm_one_grad * normal, axis=0),
            jnp.sum(norm_one_grad, axis=0),
            ffn_vectors[0, :width],
            ffn_vectors[1, :width],
            jnp.sum(cotangent.astype(F32), axis=0),
        ]
    )
    wide = lambda value: jnp.pad(value, ((0, 0), (0, 0), (0, 128 - value.shape[2])))
    features = wide(features.reshape(5, fsdp_count, shard).swapaxes(0, 1))
    query_sums = jnp.sum(query_low.astype(F32), axis=0).reshape(tp_count, -1)
    up_sums = core_order(up_shift_grad, jnp.zeros_like(up_shift_grad), axis=1)
    up_sums = jnp.stack([up_sums, jnp.zeros_like(up_sums)], axis=1).reshape(tp_count, -1)
    along = relative(jnp.concatenate([query_sums, up_sums], axis=1), 0, "tp")
    query_sums = along[:, :heads_tp].reshape(tp_count, fsdp_count, -1).swapaxes(0, 1)
    up_sums = along[:, heads_tp:].reshape(tp_count, fsdp_count, -1).swapaxes(0, 1)
    kv_sums = jnp.sum(kv_low_grad.astype(F32), axis=0).reshape(fsdp_count, 1, -1)
    vectors = jnp.concatenate(
        [
            grad_kv_mat.reshape(fsdp_count, shard, -1),
            features,
            wide(query_sums),
            wide(up_sums),
            wide(kv_sums),
        ],
        axis=1,
    )
    vectors = relative(vectors.reshape(chips, -1), 0, "fsdp").reshape(vectors.shape)
    lines = vectors.shape[1]
    vectors = vectors.reshape(chips, 2, lines, 128)
    vectors = pick(vectors[:, 0], vectors[:, 1]) + swap_fsdp(pick(vectors[:, 1], vectors[:, 0]), 1)
    for bit in reversed(bits_of(fsdp_count)[1:]):
        half = vectors.shape[0] // 2
        vectors = vectors[:half] + swap_fsdp(vectors[half:], bit)
    for bit in bits_of(tp_count):
        vectors = vectors + swap_tp(vectors, bit)
    part_tp, vectors = lax.optimization_barrier((part_tp, vectors))
    part = part[:, :2] + part_tp.astype(F32)
    branch = part[0].reshape(rows, width)
    norm_two_grad = part[1].reshape(rows, width)
    output = (inputs + attended_out + out_shift + branch + down_shift).astype(BF)
    scaled = norm_one_grad * gain_one + norm_two_grad * gain_two
    input_grad = (
        cotangent.astype(F32)
        + inverse
        * (
            scaled
            - jnp.mean(scaled, axis=-1, keepdims=True)
            - normal * jnp.mean(scaled * normal, axis=-1, keepdims=True)
        )
    ).astype(BF)

    vectors = vectors[0]
    features = vectors[shard : shard + 5, :shard]
    tail = vectors[shard + 5 :]
    query_bias_sum = lax.dynamic_slice_in_dim(tail, rank, 1, 0)[:, : query_bias.shape[1]]
    up_bias_sum = lax.dynamic_slice_in_dim(tail, tp_count + rank, 1, 0)[:, : up_bias.shape[1]]
    return (
        output,
        key_cache,
        input_grad,
        features[0],
        features[1],
        features[2],
        features[3],
        query_mat_sum,
        query_bias_sum,
        vectors[:shard],
        tail[2 * tp_count, : kv_bias.shape[0]],
        out_mat_sum,
        features[4],
        up_mat_sum,
        up_bias_sum,
        down_mat_sum,
        features[4],
    )


def solution(mesh):
    rows = P(("fsdp", "tp"), None)
    one = P("fsdp")
    tall = P("fsdp", "tp")
    turned = P("tp", "fsdp")
    lone = P("fsdp", None)
    return jax.shard_map(
        body,
        mesh=mesh,
        in_specs=(
            *(rows, rows, one, lone, one, one, one, one, tall, turned),
            *(lone, one, turned, one, tall, turned, turned, one),
        ),
        out_specs=(
            *(rows, rows, rows, one, one, one, one, tall, turned),
            *(lone, one, turned, one, tall, turned, turned, one),
        ),
        check_vma=False,
    )
```

profile of v0, /device:TPU:0, one launch (start us, length us, event | category | flops | bytes accessed | tf_op | source)
XLA Modules:
  0.0 284.4 jit_solution(13881552393164412558)
XLA Ops:
  0.7 1.7 copy.66.down
  3.0 2.2 shard_map.305
  11.3 2.6 collective-permute-start.1
  13.9 2.5 collective-permute-done.1
  16.4 1.8 collective-permute-start.2
  18.5 2.7 collective-permute-start.4
  22.9 2.7 collective-permute-start.10
  27.8 1.6 collective-permute-start.5
  30.1 2.9 %collective-permute-done.5 = bf16[192,384]{1,0:T(8,128)(2,1)S(1)} collective-permute-done((bf16[192,384]{1,0:T(8,128)(2,1)S(1)}, bf16[192,384]{1,0:T(8,128)(2,1)S(1)}, u32[]{:S(2)}, u32[]{:S(2)}) %collective-permute-start.5) | collective-permute-done | bytes 147488 | tf_op jit(solution)/shard_map/ppermute | solution.py:36
  33.2 2.5 collective-permute-start.8
  39.6 3.9 %collective-permute-done.8.refs_3_ = bf16[192,768]{1,0:T(8,128)(2,1)} collective-permute-done((bf16[192,768]{1,0:T(8,128)(2,1)S(1)}, bf16[192,768]{1,0:T(8,128)(2,1)}, u32[]{:S(2)}, u32[]{:S(2)}) %collective-permute-start.8) | collective-permute-done | bytes 294944 | tf_op jit(solution)/shard_map/ppermute | solution.py:36
  43.5 3.0 %collective-permute-done.7.refs_2_ = bf16[192,768]{1,0:T(8,128)(2,1)} collective-permute-done((bf16[192,768]{1,0:T(8,128)(2,1)S(1)}, bf16[192,768]{1,0:T(8,128)(2,1)}, u32[]{:S(2)}, u32[]{:S(2)}) %collective-permute-start.7) | collective-permute-done | bytes 294944 | tf_op jit(solution)/shard_map/ppermute | solution.py:36
  46.6 2.4 shard_map.306
  49.9 1.6 collective-permute-start.13
  53.1 8.7 %collective-permute-done.13 = bf16[896,128]{1,0:T(8,128)(2,1)S(1)} collective-permute-done((bf16[896,128]{1,0:T(8,128)(2,1)S(1)}, bf16[896,128]{1,0:T(8,128)(2,1)S(1)}, u32[]{:S(2)}, u32[]{:S(2)}) %collective-permute-start.13) | collective-permute-done | bytes 229408 | tf_op jit(solution)/shard_map/ppermute | solution.py:36
  61.9 6.1 %collective-permute-done.20 = bf16[192,768]{1,0:T(8,128)(2,1)S(1)} collective-permute-done((bf16[192,768]{1,0:T(8,128)(2,1)S(1)}, bf16[192,768]{1,0:T(8,128)(2,1)S(1)}, u32[]{:S(2)}, u32[]{:S(2)}) %collective-permute-start.20) | collective-permute-done | bytes 294944 | tf_op jit(solution)/shard_map/ppermute | solution.py:36
  68.1 2.0 fusion.18.refs_2_
  70.9 35.4 %shard_map.307 = (bf16[448,768]{1,0:T(8,128)(2,1)S(1)}, bf16[448,768]{1,0:T(8,128)(2,1)S(1)}, f32[1792,128]{1,0:T(8,128)S(1)}) custom-call(s32[7,3]{1,0:T(8,128)S(1)} %pad_add_fusion.refs_0_, f32[448,768]{1,0:T(8,128)S(1)} %convolution_add_fusion.1.refs_1_, bf16[448,768]{1,0:T(8,128)(2,1)S(1)} %fusion.18.refs_2_, ...), custom_call_target="tpu_custom_call" | custom-call | flops 15099494400 | bytes 688128 | tf_op jit(solution)/shard_map/pallas_call | solution.py:290
  106.4 14.6 %shard_map.308 = (bf16[448,768]{1,0:T(8,128)(2,1)S(1)}, bf16[448,768]{1,0:T(8,128)(2,1)S(1)}, f32[1792,128]{1,0:T(8,128)S(1)}) custom-call(s32[7,3]{1,0:T(8,128)S(1)} %pad_add_fusion.refs_0_, f32[448,768]{1,0:T(8,128)S(1)} %convolution_add_fusion.1.refs_1_, bf16[448,768]{1,0:T(8,128)(2,1)S(1)} %fusion.18.refs_2_, ...), custom_call_target="tpu_custom_call", output_to_operand_aliasing={{0}: (7, {}), {1}: (8, {})} | custom-call | flops 6039797760 | bytes 688128 | tf_op jit(solution)/shard_map/pallas_call | solution.py:290
  121.1 2.0 collective-permute-start.26
  124.1 1.7 collective-permute-start.23
  125.7 2.3 collective-permute-done.26
  128.2 1.8 collective-permute-start.27
  130.2 4.9 %shard_map.310 = (bf16[4,192,768]{2,1,0:T(8,128)(2,1)}, bf16[4,192,768]{2,1,0:T(8,128)(2,1)}) custom-call(s32[2]{0:T(128)} %pad_add_fusion.1.place.refs_0_, bf16[448,768]{1,0:T(8,128)(2,1)} %copy-done.5, bf16[448,768]{1,0:T(8,128)(2,1)} %copy-done, bf16[448,768]{1,0:T(8,128)(2,1)} %grad.1, bf16[448,768]{1,0:T(8,128)(2,1)} %copy-done.2), custom_call_target="tpu_custom_call" | custom-call | flops 1056964608 | bytes 1048576 | tf_op jit(solution)/shard_map/pallas_call | solution.py:323
  141.0 2.8 fusion.11
  144.5 10.1 %collective-permute-done.22.refs_14_ = bf16[192,1536]{1,0:T(8,128)(2,1)} collective-permute-done((bf16[192,1536]{1,0:T(8,128)(2,1)}, bf16[192,1536]{1,0:T(8,128)(2,1)}, u32[]{:S(2)}, u32[]{:S(2)}) %collective-permute-start.22) | collective-permute-done | bytes 589856 | tf_op jit(solution)/shard_map/ppermute | solution.py:36
  154.7 23.4 %shard_map.309 = (bf16[2,4,224,768]{3,2,1,0:T(8,128)(2,1)}, bf16[2,4,224,768]{3,2,1,0:T(8,128)(2,1)}, f32[8,768]{1,0:T(8,128)}, bf16[2,192,768]{2,1,0:T(8,128)(2...) custom-call(s32[2]{0:T(128)} %pad_add_fusion.1.place.refs_0_, ...), custom_call_target="tpu_custom_call" | custom-call | flops 12683575296 | bytes 1048576 | tf_op jit(solution)/shard_map/pallas_call | solution.py:323
  182.7 1.7 collective-permute-start.29
  184.3 3.6 %collective-permute-done.29 = f32[2,110,128]{2,1,0:T(8,128)S(1)} collective-permute-done((f32[2,110,128]{2,1,0:T(8,128)S(1)}, f32[2,110,128]{2,1,0:T(8,128)S(1)}, u32[]{:S(2)}, u32[]{:S(2)}) %collective-permute-start.29) | collective-permute-done | bytes 112672 | tf_op jit(solution)/shard_map/ppermute | solution.py:36
  187.9 1.6 collective-permute-start.30
  189.6 2.6 collective-permute-done.30
  192.2 1.8 collective-permute-start.31
  196.4 2.3 collective-permute-start.32
  198.8 1.6 add_convert_fusion
  201.8 2.0 collective-permute-start.36
  203.8 6.6 %collective-permute-done.41 = bf16[2,192,768]{2,1,0:T(8,128)(2,1)S(1)} collective-permute-done((bf16[2,192,768]{2,1,0:T(8,128)(2,1)}, bf16[2,192,768]{2,1,0:T(8,128)(2,1)S(1)}, u32[]{:S(2)}, u32[]{:S(2)}) %collective-permute-start.41) | collective-permute-done | bytes 589856 | tf_op jit(solution)/shard_map/ppermute | solution.py:36
  213.1 3.7 %collective-permute-done.34 = bf16[2,192,384]{2,1,0:T(8,128)(2,1)S(1)} collective-permute-done((bf16[2,192,384]{2,1,0:T(8,128)(2,1)S(1)}, bf16[2,192,384]{2,1,0:T(8,128)(2,1)S(1)}, u32[]{:S(2)}, u32[]{:S(2)}) %collective-permute-start.34) | collective-permute-done | bytes 294944 | tf_op jit(solution)/shard_map/ppermute | solution.py:36
  219.6 2.5 collective-permute-done.42
  225.3 6.1 %collective-permute-done.38 = bf16[192,384]{1,0:T(8,128)(2,1)S(1)} collective-permute-done((bf16[192,384]{1,0:T(8,128)(2,1)S(1)}, bf16[192,384]{1,0:T(8,128)(2,1)S(1)}, u32[]{:S(2)}, u32[]{:S(2)}) %collective-permute-start.38) | collective-permute-done | bytes 147488 | tf_op jit(solution)/shard_map/ppermute | solution.py:36
  231.5 2.2 collective-permute-start.39
  234.6 4.4 %collective-permute-done.39 = bf16[192,192]{1,0:T(8,128)(2,1)S(1)} collective-permute-done((bf16[192,192]{1,0:T(8,128)(2,1)S(1)}, bf16[192,192]{1,0:T(8,128)(2,1)S(1)}, u32[]{:S(2)}, u32[]{:S(2)}) %collective-permute-start.39) | collective-permute-done | bytes 73760 | tf_op jit(solution)/shard_map/ppermute | solution.py:36
  239.7 2.3 copy-done.4
  243.4 2.0 collective-permute-done.45
  249.5 22.1 %collective-permute-done.25 = bf16[2,2,224,768]{3,2,1,0:T(8,128)(2,1)S(1)} collective-permute-done((bf16[2,2,224,768]{3,2,1,0:T(8,128)(2,1)}, bf16[2,2,224,768]{3,2,1,0:T(8,128)(2,1)S(1)}, u32[]{:S(2)}, u32[]{:S(2)}) %collective-permute-start.25) | collective-permute-done | bytes 1376288 | tf_op jit(solution)/shard_map/ppermute | solution.py:36
  272.2 2.1 slice_add_fusion
  275.3 1.7 fusion.67
  277.6 2.6 fusion.16
  280.7 3.1 %fusion.17 = bf16[448,768]{1,0:T(8,128)(2,1)} fusion(f32[448,768]{1,0:T(8,128)S(1)} %bitcast.98, bf16[448,768]{1,0:T(8,128)(2,1)S(1)} %copy-done.3, bf16[448,768]{1,0:T(8,128)(2,1)} %refs_4_, f32[768]{0:T(1024)S(1)} %reshape.602, f32[768]{0:T(1024)S(1)} %reshape.599, bf16[768,768]{1,0:T(8,128)(2,1)} %collective-permute-done.9, ...), kind=kOutput, calls=%fused_computation.32 | convolution fusion | flops 531136512 | bytes 5806081 | tf_op jit(solution)/shard_map/dot_general | solution.py:25
  (267 shorter events, 53.7 us)
Async XLA Ops:
  5.2 6.0 %collective-permute-start = (bf16[1,112,128]{2,1,0:T(8,128)(2,1)}, bf16[1,112,128]{2,1,0:T(8,128)(2,1)S(1)}, u32[]{:S(2)}, u32[]{:S(2)}) collective-permute-start(bf16[1,112,128]{2,1,0:T(8,128)(2,1)} %bitcast.100), channel_id=1, source_target_pairs={{0,4},{4,0},{8,12},{12,8},{16,20},{20,16},{24,28},{28,24},{1,5},{5... | collective-permute-start | bytes 86024 | tf_op jit(solution)/shard_map/ppermute | solution.py:36
  5.8 12.5 %collective-permute-start.3 = (bf16[96,960]{1,0:T(8,128)(2,1)}, bf16[96,960]{1,0:T(8,128)(2,1)S(1)}, u32[]{:S(2)}, u32[]{:S(2)}) collective-permute-start(bf16[96,960]{1,0:T(8,128)(2,1)} %get-tuple-element.52), channel_id=1, source_target_pairs={{0,4},{4,0},{8,12},{12,8},{16,20},{20,16},{24,28},{28,24},{1,5},{5... | collective-permute-start | bytes 552968 | tf_op jit(solution)/shard_map/ppermute | solution.py:36
  5.8 133.1 %collective-permute-start.18 = (bf16[448,768]{1,0:T(8,128)(2,1)}, bf16[448,768]{1,0:T(8,128)(2,1)}, u32[]{:S(2)}, u32[]{:S(2)}) collective-permute-start(bf16[448,768]{1,0:T(8,128)(2,1)} %grad.1), channel_id=1, source_target_pairs={{0,4},{4,0},{8,12},{12,8},{16,20},{20,16},{24,28},{28,24},{1,5},{5... | collective-permute-start | bytes 2064392 | tf_op jit(solution)/shard_map/ppermute | solution.py:36
  11.3 5.1 %collective-permute-start.1 = (bf16[2,112,128]{2,1,0:T(8,128)(2,1)S(1)}, bf16[2,112,128]{2,1,0:T(8,128)(2,1)S(1)}, u32[]{:S(2)}, u32[]{:S(2)}) collective-permute-start(bf16[2,112,128]{2,1,0:T(8,128)(2,1)S(1)} %maximum_select_fusion.3), channel_id=1, source_target_pairs={{0,8},{4,12},{8,0},{12,4},{16,24},{20,28},{24,16},{28,20},{1,9},{5... | collective-permute-start | bytes 172040 | tf_op jit(solution)/shard_map/ppermute | solution.py:36
  16.4 5.0 %collective-permute-start.2 = (bf16[4,112,128]{2,1,0:T(8,128)(2,1)S(1)}, bf16[4,112,128]{2,1,0:T(8,128)(2,1)S(1)}, u32[]{:S(2)}, u32[]{:S(2)}) collective-permute-start(bf16[4,112,128]{2,1,0:T(8,128)(2,1)S(1)} %pad_maximum_fusion.11), channel_id=1, source_target_pairs={{0,16},{4,20},{8,24},{12,28},{16,0},{20,4},{24,8},{28,12},{1,17},{... | collective-permute-start | bytes 344072 | tf_op jit(solution)/shard_map/ppermute | solution.py:36
  18.5 9.1 %collective-permute-start.4 = (bf16[192,192]{1,0:T(8,128)(2,1)S(1)}, bf16[192,192]{1,0:T(8,128)(2,1)S(1)}, u32[]{:S(2)}, u32[]{:S(2)}) collective-permute-start(bf16[192,192]{1,0:T(8,128)(2,1)S(1)} %slice.482), channel_id=1, source_target_pairs={{0,2},{1,3},{2,0},{3,1},{4,6},{5,7},{6,4},{7,5},{8,10},{9,11},{10,... | collective-permute-start | bytes 221192 | tf_op jit(solution)/shard_map/ppermute | solution.py:36
  22.9 6.7 %collective-permute-start.10 = (bf16[1,576]{1,0:T(2,128)(2,1)S(1)}, bf16[1,576]{1,0:T(2,128)(2,1)S(1)}, u32[]{:S(2)}, u32[]{:S(2)}) collective-permute-start(bf16[1,576]{1,0:T(2,128)(2,1)S(1)} %pad_maximum_fusion.17), channel_id=1, source_target_pairs={{0,2},{1,3},{2,0},{3,1},{4,6},{5,7},{6,4},{7,5},{8,10},{9,11},{10,... | collective-permute-start | bytes 3464 | tf_op jit(solution)/shard_map/ppermute | solution.py:36
  27.2 43.0 %copy-start.5 = (bf16[448,768]{1,0:T(8,128)(2,1)}, bf16[448,768]{1,0:T(8,128)(2,1)S(1)}, u32[]{:S(2)}) copy-start(bf16[448,768]{1,0:T(8,128)(2,1)S(1)} %fusion.10.one) | copy-start | bytes 2064388
  27.8 5.2 %collective-permute-start.5 = (bf16[192,384]{1,0:T(8,128)(2,1)S(1)}, bf16[192,384]{1,0:T(8,128)(2,1)S(1)}, u32[]{:S(2)}, u32[]{:S(2)}) collective-permute-start(bf16[192,384]{1,0:T(8,128)(2,1)S(1)} %pad_maximum_fusion.9), channel_id=1, source_target_pairs={{0,1},{1,0},{2,3},{3,2},{4,5},{5,4},{6,7},{7,6},{8,9},{9,8},{10,11... | collective-permute-start | bytes 442376 | tf_op jit(solution)/shard_map/ppermute | solution.py:36
  29.6 9.7 %collective-permute-start.11 = (bf16[2,576]{1,0:T(2,128)(2,1)S(1)}, bf16[2,576]{1,0:T(2,128)(2,1)S(1)}, u32[]{:S(2)}, u32[]{:S(2)}) collective-permute-start(bf16[2,576]{1,0:T(2,128)(2,1)S(1)} %pad_maximum_fusion.18), channel_id=1, source_target_pairs={{0,1},{1,0},{2,3},{3,2},{4,5},{5,4},{6,7},{7,6},{8,9},{9,8},{10,11... | collective-permute-start | bytes 6920 | tf_op jit(solution)/shard_map/ppermute | solution.py:36
  33.2 10.3 %collective-permute-start.8 = (bf16[192,768]{1,0:T(8,128)(2,1)S(1)}, bf16[192,768]{1,0:T(8,128)(2,1)}, u32[]{:S(2)}, u32[]{:S(2)}) collective-permute-start(bf16[192,768]{1,0:T(8,128)(2,1)S(1)} %pad_maximum_fusion.4.refs_0_), channel_id=1, source_target_pairs={{0,24},{4,28},{8,16},{12,20},{16,8},{20,12},{24,0},{28,4},{1,25},{... | collective-permute-start | bytes 884744 | tf_op jit(solution)/shard_map/ppermute | solution.py:36
  35.7 10.8 %collective-permute-start.7 = (bf16[192,768]{1,0:T(8,128)(2,1)S(1)}, bf16[192,768]{1,0:T(8,128)(2,1)}, u32[]{:S(2)}, u32[]{:S(2)}) collective-permute-start(bf16[192,768]{1,0:T(8,128)(2,1)S(1)} %pad_maximum_fusion.4.refs_0_), channel_id=1, source_target_pairs={{0,16},{4,20},{8,24},{12,28},{16,0},{20,4},{24,8},{28,12},{1,17},{... | collective-permute-start | bytes 884744 | tf_op jit(solution)/shard_map/ppermute | solution.py:36
  36.3 10.4 %collective-permute-start.6 = (bf16[192,768]{1,0:T(8,128)(2,1)S(1)}, bf16[192,768]{1,0:T(8,128)(2,1)}, u32[]{:S(2)}, u32[]{:S(2)}) collective-permute-start(bf16[192,768]{1,0:T(8,128)(2,1)S(1)} %pad_maximum_fusion.4.refs_0_), channel_id=1, source_target_pairs={{0,8},{4,12},{8,0},{12,4},{16,24},{20,28},{24,16},{28,20},{1,9},{5... | collective-permute-start | bytes 884744 | tf_op jit(solution)/shard_map/ppermute | solution.py:36
  39.3 10.5 %collective-permute-start.12 = (bf16[448,128]{1,0:T(8,128)(2,1)S(1)}, bf16[448,128]{1,0:T(8,128)(2,1)S(1)}, u32[]{:S(2)}, u32[]{:S(2)}) collective-permute-start(bf16[448,128]{1,0:T(8,128)(2,1)S(1)} %get-tuple-element.258), channel_id=1, source_target_pairs={{0,2},{1,3},{2,0},{3,1},{4,6},{5,7},{6,4},{7,5},{8,10},{9,11},{10,... | collective-permute-start | bytes 344072 | tf_op jit(solution)/shard_map/ppermute | solution.py:36
  43.5 95.9 %collective-permute-start.16 = (bf16[448,768]{1,0:T(8,128)(2,1)}, bf16[448,768]{1,0:T(8,128)(2,1)}, u32[]{:S(2)}, u32[]{:S(2)}) collective-permute-start(bf16[448,768]{1,0:T(8,128)(2,1)} %refs_4_), channel_id=1, source_target_pairs={{0,4},{4,0},{8,12},{12,8},{16,20},{20,16},{24,28},{28,24},{1,5},{5... | collective-permute-start | bytes 2064392 | tf_op jit(solution)/shard_map/ppermute | solution.py:36
  49.0 19.1 %collective-permute-start.9 = (bf16[768,768]{1,0:T(8,128)(2,1)}, bf16[768,768]{1,0:T(8,128)(2,1)}, u32[]{:S(2)}, u32[]{:S(2)}) collective-permute-start(bf16[768,768]{1,0:T(8,128)(2,1)} %shard_map.306), channel_id=1, source_target_pairs={{0,4},{4,0},{8,12},{12,8},{16,20},{20,16},{24,28},{28,24},{1,5},{5... | collective-permute-start | bytes 3538952 | tf_op jit(solution)/shard_map/ppermute | solution.py:36
  49.9 12.0 %collective-permute-start.13 = (bf16[896,128]{1,0:T(8,128)(2,1)S(1)}, bf16[896,128]{1,0:T(8,128)(2,1)S(1)}, u32[]{:S(2)}, u32[]{:S(2)}) collective-permute-start(bf16[896,128]{1,0:T(8,128)(2,1)S(1)} %pad_maximum_fusion.7), channel_id=1, source_target_pairs={{0,1},{1,0},{2,3},{3,2},{4,5},{5,4},{6,7},{7,6},{8,9},{9,8},{10,11... | collective-permute-start | bytes 688136 | tf_op jit(solution)/shard_map/ppermute | solution.py:36
  51.5 16.5 %collective-permute-start.20 = (bf16[192,768]{1,0:T(8,128)(2,1)S(1)}, bf16[192,768]{1,0:T(8,128)(2,1)S(1)}, u32[]{:S(2)}, u32[]{:S(2)}) collective-permute-start(bf16[192,768]{1,0:T(8,128)(2,1)S(1)} %slice.500), channel_id=1, source_target_pairs={{0,2},{1,3},{2,0},{3,1},{4,6},{5,7},{6,4},{7,5},{8,10},{9,11},{10,... | collective-permute-start | bytes 884744 | tf_op jit(solution)/shard_map/ppermute | solution.py:36
  61.8 44.5 %collective-permute-start.14 = (bf16[448,768]{1,0:T(8,128)(2,1)}, bf16[448,768]{1,0:T(8,128)(2,1)}, u32[]{:S(2)}, u32[]{:S(2)}) collective-permute-start(bf16[448,768]{1,0:T(8,128)(2,1)} %refs_4_), channel_id=1, source_target_pairs={{0,1},{1,0},{2,3},{3,2},{4,5},{5,4},{6,7},{7,6},{8,9},{9,8},{10,11... | collective-permute-start | bytes 2064392 | tf_op jit(solution)/shard_map/ppermute | solution.py:36
  68.0 38.4 %collective-permute-start.15 = (bf16[448,768]{1,0:T(8,128)(2,1)S(1)}, bf16[448,768]{1,0:T(8,128)(2,1)}, u32[]{:S(2)}, u32[]{:S(2)}) collective-permute-start(bf16[448,768]{1,0:T(8,128)(2,1)S(1)} %copy-done.8), channel_id=1, source_target_pairs={{0,1},{1,0},{2,3},{3,2},{4,5},{5,4},{6,7},{7,6},{8,9},{9,8},{10,11... | collective-permute-start | bytes 2064392 | tf_op jit(solution)/shard_map/ppermute | solution.py:36
  121.1 6.9 %collective-permute-start.26 = (bf16[896,128]{1,0:T(8,128)(2,1)S(1)}, bf16[896,128]{1,0:T(8,128)(2,1)S(1)}, u32[]{:S(2)}, u32[]{:S(2)}) collective-permute-start(bf16[896,128]{1,0:T(8,128)(2,1)S(1)} %pad_maximum_fusion.8), channel_id=1, source_target_pairs={{0,1},{1,0},{2,3},{3,2},{4,5},{5,4},{6,7},{7,6},{8,9},{9,8},{10,11... | collective-permute-start | bytes 688136 | tf_op jit(solution)/shard_map/ppermute | solution.py:36
  124.1 20.3 %collective-permute-start.23 = (bf16[192,1536]{1,0:T(8,128)(2,1)}, bf16[192,1536]{1,0:T(8,128)(2,1)}, u32[]{:S(2)}, u32[]{:S(2)}) collective-permute-start(bf16[192,1536]{1,0:T(8,128)(2,1)} %pad_maximum_fusion.refs_12_), channel_id=1, source_target_pairs={{0,24},{4,28},{8,16},{12,20},{16,8},{20,12},{24,0},{28,4},{1,25},{... | collective-permute-start | bytes 1769480 | tf_op jit(solution)/shard_map/ppermute | solution.py:36
  128.2 7.0 %collective-permute-start.27 = (bf16[448,128]{1,0:T(8,128)(2,1)S(1)}, bf16[448,128]{1,0:T(8,128)(2,1)S(1)}, u32[]{:S(2)}, u32[]{:S(2)}) collective-permute-start(bf16[448,128]{1,0:T(8,128)(2,1)S(1)} %fusion.30), channel_id=1, source_target_pairs={{0,2},{1,3},{2,0},{3,1},{4,6},{5,7},{6,4},{7,5},{8,10},{9,11},{10,... | collective-permute-start | bytes 344072 | tf_op jit(solution)/shard_map/ppermute | solution.py:36
  130.2 24.5 %collective-permute-start.17 = (bf16[448,768]{1,0:T(8,128)(2,1)}, bf16[448,768]{1,0:T(8,128)(2,1)}, u32[]{:S(2)}, u32[]{:S(2)}) collective-permute-start(bf16[448,768]{1,0:T(8,128)(2,1)} %collective-permute-done.14.refs_5_), channel_id=1, source_target_pairs={{0,4},{4,0},{8,12},{12,8},{16,20},{20,16},{24,28},{28,24},{1,5},{5... | collective-permute-start | bytes 2064392 | tf_op jit(solution)/shard_map/ppermute | solution.py:36
  135.1 19.6 %collective-permute-start.19 = (bf16[448,768]{1,0:T(8,128)(2,1)}, bf16[448,768]{1,0:T(8,128)(2,1)}, u32[]{:S(2)}, u32[]{:S(2)}) collective-permute-start(bf16[448,768]{1,0:T(8,128)(2,1)} %collective-permute-done.15.refs_9_), channel_id=1, source_target_pairs={{0,4},{4,0},{8,12},{12,8},{16,20},{20,16},{24,28},{28,24},{1,5},{5... | collective-permute-start | bytes 2064392 | tf_op jit(solution)/shard_map/ppermute | solution.py:36
  138.9 15.6 %collective-permute-start.22 = (bf16[192,1536]{1,0:T(8,128)(2,1)}, bf16[192,1536]{1,0:T(8,128)(2,1)}, u32[]{:S(2)}, u32[]{:S(2)}) collective-permute-start(bf16[192,1536]{1,0:T(8,128)(2,1)} %pad_maximum_fusion.refs_12_), channel_id=1, source_target_pairs={{0,16},{4,20},{8,24},{12,28},{16,0},{20,4},{24,8},{28,12},{1,17},{... | collective-permute-start | bytes 1769480 | tf_op jit(solution)/shard_map/ppermute | solution.py:36
  139.4 15.3 %collective-permute-start.21 = (bf16[192,1536]{1,0:T(8,128)(2,1)}, bf16[192,1536]{1,0:T(8,128)(2,1)}, u32[]{:S(2)}, u32[]{:S(2)}) collective-permute-start(bf16[192,1536]{1,0:T(8,128)(2,1)} %pad_maximum_fusion.refs_12_), channel_id=1, source_target_pairs={{0,8},{4,12},{8,0},{12,4},{16,24},{20,28},{24,16},{28,20},{1,9},{5... | collective-permute-start | bytes 1769480 | tf_op jit(solution)/shard_map/ppermute | solution.py:36
  144.4 54.4 %collective-permute-start.33 = (bf16[4,192,768]{2,1,0:T(8,128)(2,1)}, bf16[4,192,768]{2,1,0:T(8,128)(2,1)}, u32[]{:S(2)}, u32[]{:S(2)}) collective-permute-start(bf16[4,192,768]{2,1,0:T(8,128)(2,1)} %get-tuple-element.78), channel_id=1, source_target_pairs={{0,4},{4,0},{8,12},{12,8},{16,20},{20,16},{24,28},{28,24},{1,5},{5... | collective-permute-start | bytes 3538952 | tf_op jit(solution)/shard_map/ppermute | solution.py:36
  181.0 1.6 collective-permute-start.28
  182.7 5.3 %collective-permute-start.29 = (f32[2,110,128]{2,1,0:T(8,128)S(1)}, f32[2,110,128]{2,1,0:T(8,128)S(1)}, u32[]{:S(2)}, u32[]{:S(2)}) collective-permute-start(f32[2,110,128]{2,1,0:T(8,128)S(1)} %slice.527), channel_id=1, source_target_pairs={{0,16},{4,20},{8,24},{12,28},{16,0},{20,4},{24,8},{28,12},{1,17},{... | collective-permute-start | bytes 337928 | tf_op jit(solution)/shard_map/ppermute | solution.py:36
  187.9 4.2 %collective-permute-start.30 = (f32[1,110,128]{2,1,0:T(8,128)S(1)}, f32[1,110,128]{2,1,0:T(8,128)S(1)}, u32[]{:S(2)}, u32[]{:S(2)}) collective-permute-start(f32[1,110,128]{2,1,0:T(8,128)S(1)} %slice.529), channel_id=1, source_target_pairs={{0,8},{4,12},{8,0},{12,4},{16,24},{20,28},{24,16},{28,20},{1,9},{5... | collective-permute-start | bytes 168968 | tf_op jit(solution)/shard_map/ppermute | solution.py:36
  192.2 4.2 %collective-permute-start.31 = (f32[1,110,128]{2,1,0:T(8,128)S(1)}, f32[1,110,128]{2,1,0:T(8,128)S(1)}, u32[]{:S(2)}, u32[]{:S(2)}) collective-permute-start(f32[1,110,128]{2,1,0:T(8,128)S(1)} %slice_add_fusion.6), channel_id=1, source_target_pairs={{0,1},{1,0},{2,3},{3,2},{4,5},{5,4},{6,7},{7,6},{8,9},{9,8},{10,11... | collective-permute-start | bytes 168968 | tf_op jit(solution)/shard_map/ppermute | solution.py:36
  194.0 16.4 %collective-permute-start.41 = (bf16[2,192,768]{2,1,0:T(8,128)(2,1)}, bf16[2,192,768]{2,1,0:T(8,128)(2,1)S(1)}, u32[]{:S(2)}, u32[]{:S(2)}) collective-permute-start(bf16[2,192,768]{2,1,0:T(8,128)(2,1)} %get-tuple-element.80), channel_id=1, source_target_pairs={{0,8},{4,12},{8,0},{12,4},{16,24},{20,28},{24,16},{28,20},{1,9},{5... | collective-permute-start | bytes 1769480 | tf_op jit(solution)/shard_map/ppermute | solution.py:36
  194.9 16.4 %collective-permute-start.43 = (bf16[2,192,768]{2,1,0:T(8,128)(2,1)}, bf16[2,192,768]{2,1,0:T(8,128)(2,1)S(1)}, u32[]{:S(2)}, u32[]{:S(2)}) collective-permute-start(bf16[2,192,768]{2,1,0:T(8,128)(2,1)} %get-tuple-element.82), channel_id=1, source_target_pairs={{0,16},{4,20},{8,24},{12,28},{16,0},{20,4},{24,8},{28,12},{1,17},{... | collective-permute-start | bytes 1769480 | tf_op jit(solution)/shard_map/ppermute | solution.py:36
  196.3 42.7 %collective-permute-start.24 = (bf16[2,4,224,768]{3,2,1,0:T(8,128)(2,1)}, bf16[2,4,224,768]{3,2,1,0:T(8,128)(2,1)S(1)}, u32[]{:S(2)}, u32[]{:S(2)}) collective-permute-start(bf16[2,4,224,768]{3,2,1,0:T(8,128)(2,1)} %get-tuple-element.71), channel_id=1, source_target_pairs={{0,4},{4,0},{8,12},{12,8},{16,20},{20,16},{24,28},{28,24},{1,5},{5... | collective-permute-start | bytes 8257544 | tf_op jit(solution)/shard_map/ppermute | solution.py:36
  196.4 5.3 %collective-permute-start.32 = (f32[1,110,128]{2,1,0:T(8,128)S(1)}, f32[1,110,128]{2,1,0:T(8,128)S(1)}, u32[]{:S(2)}, u32[]{:S(2)}) collective-permute-start(f32[1,110,128]{2,1,0:T(8,128)S(1)} %add.308), channel_id=1, source_target_pairs={{0,2},{1,3},{2,0},{3,1},{4,6},{5,7},{6,4},{7,5},{8,10},{9,11},{10,... | collective-permute-start | bytes 168968 | tf_op jit(solution)/shard_map/ppermute | solution.py:36
  200.5 16.2 %collective-permute-start.34 = (bf16[2,192,384]{2,1,0:T(8,128)(2,1)S(1)}, bf16[2,192,384]{2,1,0:T(8,128)(2,1)S(1)}, u32[]{:S(2)}, u32[]{:S(2)}) collective-permute-start(bf16[2,192,384]{2,1,0:T(8,128)(2,1)S(1)} %get-tuple-element.171), channel_id=1, source_target_pairs={{0,8},{4,12},{8,0},{12,4},{16,24},{20,28},{24,16},{28,20},{1,9},{5... | collective-permute-start | bytes 884744 | tf_op jit(solution)/shard_map/ppermute | solution.py:36
  201.8 15.8 %collective-permute-start.36 = (bf16[2,192,384]{2,1,0:T(8,128)(2,1)S(1)}, bf16[2,192,384]{2,1,0:T(8,128)(2,1)S(1)}, u32[]{:S(2)}, u32[]{:S(2)}) collective-permute-start(bf16[2,192,384]{2,1,0:T(8,128)(2,1)S(1)} %get-tuple-element.172), channel_id=1, source_target_pairs={{0,16},{4,20},{8,24},{12,28},{16,0},{20,4},{24,8},{28,12},{1,17},{... | collective-permute-start | bytes 884744 | tf_op jit(solution)/shard_map/ppermute | solution.py:36
  210.6 11.5 %collective-permute-start.42 = (bf16[1,192,768]{2,1,0:T(8,128)(2,1)S(1)}, bf16[1,192,768]{2,1,0:T(8,128)(2,1)S(1)}, u32[]{:S(2)}, u32[]{:S(2)}) collective-permute-start(bf16[1,192,768]{2,1,0:T(8,128)(2,1)S(1)} %slice.554), channel_id=1, source_target_pairs={{0,16},{4,20},{8,24},{12,28},{16,0},{20,4},{24,8},{28,12},{1,17},{... | collective-permute-start | bytes 884744 | tf_op jit(solution)/shard_map/ppermute | solution.py:36
  211.5 13.7 %collective-permute-start.44 = (bf16[1,192,768]{2,1,0:T(8,128)(2,1)S(1)}, bf16[1,192,768]{2,1,0:T(8,128)(2,1)S(1)}, u32[]{:S(2)}, u32[]{:S(2)}) collective-permute-start(bf16[1,192,768]{2,1,0:T(8,128)(2,1)S(1)} %slice.558), channel_id=1, source_target_pairs={{0,8},{4,12},{8,0},{12,4},{16,24},{20,28},{24,16},{28,20},{1,9},{5... | collective-permute-start | bytes 884744 | tf_op jit(solution)/shard_map/ppermute | solution.py:36
  217.8 5.3 %collective-permute-start.37 = (bf16[1,192,384]{2,1,0:T(8,128)(2,1)S(1)}, bf16[1,192,384]{2,1,0:T(8,128)(2,1)S(1)}, u32[]{:S(2)}, u32[]{:S(2)}) collective-permute-start(bf16[1,192,384]{2,1,0:T(8,128)(2,1)S(1)} %slice.544), channel_id=1, source_target_pairs={{0,8},{4,12},{8,0},{12,4},{16,24},{20,28},{24,16},{28,20},{1,9},{5... | collective-permute-start | bytes 442376 | tf_op jit(solution)/shard_map/ppermute | solution.py:36
  219.3 5.1 %collective-permute-start.35 = (bf16[1,192,384]{2,1,0:T(8,128)(2,1)S(1)}, bf16[1,192,384]{2,1,0:T(8,128)(2,1)S(1)}, u32[]{:S(2)}, u32[]{:S(2)}) collective-permute-start(bf16[1,192,384]{2,1,0:T(8,128)(2,1)S(1)} %slice.538), channel_id=1, source_target_pairs={{0,16},{4,20},{8,24},{12,28},{16,0},{20,4},{24,8},{28,12},{1,17},{... | collective-permute-start | bytes 442376 | tf_op jit(solution)/shard_map/ppermute | solution.py:36
  224.7 6.7 %collective-permute-start.38 = (bf16[192,384]{1,0:T(8,128)(2,1)S(1)}, bf16[192,384]{1,0:T(8,128)(2,1)S(1)}, u32[]{:S(2)}, u32[]{:S(2)}) collective-permute-start(bf16[192,384]{1,0:T(8,128)(2,1)S(1)} %pad_maximum_fusion.10), channel_id=1, source_target_pairs={{0,1},{1,0},{2,3},{3,2},{4,5},{5,4},{6,7},{7,6},{8,9},{9,8},{10,11... | collective-permute-start | bytes 442376 | tf_op jit(solution)/shard_map/ppermute | solution.py:36
  231.5 7.5 %collective-permute-start.39 = (bf16[192,192]{1,0:T(8,128)(2,1)S(1)}, bf16[192,192]{1,0:T(8,128)(2,1)S(1)}, u32[]{:S(2)}, u32[]{:S(2)}) collective-permute-start(bf16[192,192]{1,0:T(8,128)(2,1)S(1)} %fusion.38), channel_id=1, source_target_pairs={{0,2},{1,3},{2,0},{3,1},{4,6},{5,7},{6,4},{7,5},{8,10},{9,11},{10,... | collective-permute-start | bytes 221192 | tf_op jit(solution)/shard_map/ppermute | solution.py:36
  233.7 11.7 %collective-permute-start.45 = (bf16[192,768]{1,0:T(8,128)(2,1)S(1)}, bf16[192,768]{1,0:T(8,128)(2,1)S(1)}, u32[]{:S(2)}, u32[]{:S(2)}) collective-permute-start(bf16[192,768]{1,0:T(8,128)(2,1)S(1)} %pad_maximum_fusion.5), channel_id=1, source_target_pairs={{0,2},{1,3},{2,0},{3,1},{4,6},{5,7},{6,4},{7,5},{8,10},{9,11},{10,... | collective-permute-start | bytes 884744 | tf_op jit(solution)/shard_map/ppermute | solution.py:36
  243.3 28.3 %collective-permute-start.25 = (bf16[2,2,224,768]{3,2,1,0:T(8,128)(2,1)}, bf16[2,2,224,768]{3,2,1,0:T(8,128)(2,1)S(1)}, u32[]{:S(2)}, u32[]{:S(2)}) collective-permute-start(bf16[2,2,224,768]{3,2,1,0:T(8,128)(2,1)} %slice.816), channel_id=1, source_target_pairs={{0,1},{1,0},{2,3},{3,2},{4,5},{5,4},{6,7},{7,6},{8,9},{9,8},{10,11... | collective-permute-start | bytes 4128776 | tf_op jit(solution)/shard_map/ppermute | solution.py:36
  243.3 2.9 %collective-permute-start.40 = (f32[96,192]{1,0:T(8,128)S(1)}, f32[96,192]{1,0:T(8,128)S(1)}, u32[]{:S(2)}, u32[]{:S(2)}) collective-permute-start(f32[96,192]{1,0:T(8,128)S(1)} %slice_select_fusion.8), channel_id=1, source_target_pairs={{0,4},{4,0},{8,12},{12,8},{16,20},{20,16},{24,28},{28,24},{1,5},{5... | collective-permute-start | bytes 221192 | tf_op jit(solution)/shard_map/ppermute | solution.py:36
  246.2 1.8 collective-permute-start.46
  (21 other events, 206.8 us)
where the time goes:
time: 285 us; the launch traced here: 284 us
  waiting for transfers between devices  99.1 us (35%)
  Pallas kernels  83 us (29%)
  starting transfers between devices  48.1 us (17%)
  other arithmetic  25 us (9%)
  local copies, waits for them, and re-layouts  16.3 us (6%)
  matrix products  11.2 us (4%)
    ppermute x47, waiting for transfers between devices, swap(): return lax.ppermute(value, axis, [(i, i ^ bit) for i in range(count)])  99.1 us
    pallas_call x2, Pallas kernels, attention(): pl.pallas_call(lambda *refs: attention_kernel(first, *refs), out_shape=(j...  50.1 us
    ppermute x47, starting transfers between devices, swap(): return lax.ppermute(value, axis, [(i, i ^ bit) for i in range(count)])  48.1 us
    pallas_call x4, Pallas kernels, local_kernel(): pl.pallas_call(kernel, out_shape=[jax.ShapeDtypeStruct(shape, kind) for s...  32.9 us
    dot_general x7, matrix products, dot(): lax.dot_general(left, right, (((left_dim,), (right_dim,)), ((), ())), pre...  10.9 us
    unnamed x50, local copies, waits for them, and re-layouts  6.02 us
  transfers between devices with their start and end apart: 47, of which 28 were waited for; matrix products, arithmetic and copies ran while one was open for 12% of the time, Pallas kernels for 28%

commit v1 on v0

--- a/solution.py
+++ b/solution.py
@@ -77,7 +77,8 @@
         bits = bits_of(lax.axis_size("fsdp"))[:0:-1]
         value = value.reshape(bits[0], -1, kept.shape[2])
     else:
-        value = add_low(kept, swap_fsdp(sent, bits[0]))
+        taken = swap_fsdp(sent, bits[0])
+        value = add_low(kept, taken)
         bits = bits[1:]
     for bit in bits:
         half = value.shape[0] // 2
@@ -166,8 +167,7 @@
         query_grads,
         keys,
         values,
-        key_acc,
-        value_acc,
+        acc,
         bias,
     ) = refs
     step = pl.program_id(0)
@@ -225,8 +225,7 @@
             queries[group, rows, :] = turned[:, side * HD : (side + 1) * HD]
             grads[group, rows, :] = grad[:, side * HD : (side + 1) * HD]
 
-    key_acc[...] = jnp.zeros_like(key_acc)
-    value_acc[...] = jnp.zeros_like(value_acc)
+    acc[...] = jnp.zeros_like(acc)
 
     def one_group(group, carry):
         query = queries[group]
@@ -245,8 +244,8 @@
         delta = jnp.sum(prob * grad_prob, axis=1, keepdims=True)
         score_grad = (prob * (grad_prob - delta)).astype(BF)
         query_grads[group] = dot(score_grad, key, 1, 0)
-        key_acc[...] += dot(score_grad, query, 0, 0)
-        value_acc[...] += dot(prob_low, grad, 0, 0)
+        acc[:HD, :] += dot(query, score_grad, 0, 0)
+        acc[HD:, :] += dot(grad, prob_low, 0, 0)
         return carry
 
     lax.fori_loop(0, groups, one_group, 0)
@@ -268,12 +267,9 @@
             - pltpu.roll(turned, 128 - ROT // 2, 1) * back
             - pltpu.roll(turned, ROT // 2, 1) * ahead
         ).astype(BF)
-    kv_grad_ref[:trunk, :HD] += key_acc[:trunk, :]
-    kv_grad_ref[:trunk, HD:] += value_acc[:trunk, :]
-    kv_grad_ref[parent_rows, :HD] += key_acc[trunk : trunk + BLK, :]
-    kv_grad_ref[parent_rows, HD:] += value_acc[trunk : trunk + BLK, :]
-    kv_grad_ref[own_rows, :HD] += key_acc[trunk + BLK :, :]
-    kv_grad_ref[own_rows, HD:] += value_acc[trunk + BLK :, :]
+    kv_grad_ref[:, :trunk] += acc[:, :trunk]
+    kv_grad_ref[:, parent_rows] += acc[:, trunk : trunk + BLK]
+    kv_grad_ref[:, own_rows] += acc[:, trunk + BLK :]
 
 
 def attention(meta, query_lin, grad_attended, key_value, cos, back, ahead, first, last, earlier):
@@ -284,7 +280,8 @@
     tile = lambda lanes: pl.BlockSpec((TILE, lanes), lambda i, m: (i + first, 0))
     whole = pl.BlockSpec(key_value.shape, lambda i, m: (0, 0))
     anywhere = pl.BlockSpec(memory_space=pl.ANY)
-    given = [] if earlier is None else [anywhere, anywhere, whole]
+    turned = pl.BlockSpec(key_value.shape[::-1], lambda i, m: (0, 0))
+    given = [] if earlier is None else [anywhere, anywhere, turned]
     count = last - first
     work = 6 * count * TILE * (width // HD) * seen
     return pl.pallas_call(
@@ -292,13 +289,13 @@
         out_shape=(
             jax.ShapeDtypeStruct((rows, width), BF),
             jax.ShapeDtypeStruct((rows, width), BF),
-            jax.ShapeDtypeStruct(key_value.shape, F32),
+            jax.ShapeDtypeStruct(key_value.shape[::-1], F32),
         ),
         grid_spec=pltpu.PrefetchScalarGridSpec(
             num_scalar_prefetch=1,
             grid=(count,),
             in_specs=[tile(width), tile(width), whole, tile(128), tile(128), tile(128)] + given,
-            out_specs=[tile(width), tile(width), whole],
+            out_specs=[tile(width), tile(width), turned],
             scratch_shapes=[
                 pltpu.VMEM((groups, stacked, HD), BF),
                 pltpu.VMEM((groups, stacked, HD), BF),
@@ -306,8 +303,7 @@
                 pltpu.VMEM((groups, stacked, HD), F32),
                 pltpu.VMEM((seen, HD), BF),
                 pltpu.VMEM((seen, HD), BF),
-                pltpu.VMEM((seen, HD), F32),
-                pltpu.VMEM((seen, HD), F32),
+                pltpu.VMEM((2 * HD, seen), F32),
                 pltpu.VMEM((TILE, seen), F32),
             ],
         ),
@@ -349,7 +345,7 @@
     half = up.shape[1] // 2
     unit = identity(shard)
     out_turned = dot(unit, out[...], 1, 1).astype(BF)
-    down_turned = dot(unit, down[...], 1, 1).astype(BF)
+    down_turned = down[...]
     first = core == 0
 
     def pair(one, two, at):
@@ -396,6 +392,45 @@
             kept[spot] = value
         else:
             sent[spot - kept.shape[0]] = value
+
+
+def finish_kernel(
+    kept, taken, from_pair, tokens, grad, base, one_grad, gain_one, gain_two, shift, out, input_grad
+):
+    part = kept[:, 0].astype(F32) + taken[:, 0].astype(F32) + from_pair[:, 0].astype(F32)
+    value = tokens[...].astype(F32)
+    out[...] = (value + base[...] + shift[...] + part[0]).astype(BF)
+    centred = value - jnp.mean(value, axis=1, keepdims=True)
+    inverse = lax.rsqrt(jnp.mean(centred * centred, axis=1, keepdims=True) + NORM_EPS)
+    normal = centred * inverse
+    scaled = one_grad[...] * gain_one[...] + part[1] * gain_two[...]
+    mean = jnp.mean(scaled, axis=1, keepdims=True)
+    along = jnp.mean(scaled * normal, axis=1, keepdims=True)
+    input_grad[...] = (
+        grad[...].astype(F32) + inverse * (scaled - mean - normal * along)
+    ).astype(BF)
+
+
+def finish(kept, taken, from_pair, tokens, grad, base, one_grad, gain_one, gain_two, shift):
+    rows, width = tokens.shape
+    half = kept.shape[2]
+    parts = pl.BlockSpec((2, 1, half, width), lambda i: (0, i, 0, 0))
+    tile = pl.BlockSpec((half, width), lambda i: (i, 0))
+    line = pl.BlockSpec((1, width), lambda i: (0, 0))
+    call = pl.pallas_call(
+        finish_kernel,
+        grid=(rows // half,),
+        out_shape=[jax.ShapeDtypeStruct((rows, width), BF)] * 2,
+        in_specs=[parts] * 3 + [tile] * 4 + [line] * 3,
+        out_specs=[tile] * 2,
+        cost_estimate=pl.CostEstimate(
+            flops=30 * rows * width, bytes_accessed=24 * rows * width, transcendentals=0
+        ),
+        name="finish",
+    )
+    return call(
+        kept, taken, from_pair, tokens, grad, base, one_grad, gain_one, gain_two, shift
+    )
 
 
 def mat_grad_kernel(place, one, query_low, grad, attended, kept, sent, first, second):
@@ -536,7 +571,7 @@
     kept, sent, small = local_kernel(
         pack_kernel,
         [((shard, packed), BF), ((shard, packed), BF), ((LINES + shard, 128), BF)],
-        [place, query_weight, out_weight, up_weight, down_weight, kv_weight, *lines],
+        [place, query_weight, out_weight, up_weight, down_weight.T, kv_weight, *lines],
         [pltpu.VMEM((LINES, 128), F32)],
     )
     small = small[None]
@@ -566,10 +601,9 @@
     query_own = line_at(7, query_bias.shape[1])
     up_own = line_at(8, up_bias.shape[1])
     up_own = pick(up_own[:, :hidden_half], up_own[:, hidden_half:])
-    shifts = jnp.concatenate(tp_gather(jnp.concatenate([query_own, up_own], axis=1), 0), axis=0)
-    shifts = shifts.astype(F32)
-    query_shift = shifts[:, :heads_tp].reshape(-1)
-    up_shift = shifts[::2, heads_tp:].reshape(1, -1)
+    shift_own = jnp.concatenate([query_own, up_own], axis=1)
+    shift_size = shift_own.shape[1]
+    shift_own = jnp.pad(shift_own, ((0, 0), (0, -shift_size % 2048))).reshape(-1, 128)
 
     inputs = tokens.astype(F32)
     centred = inputs - jnp.mean(inputs, axis=-1, keepdims=True)
@@ -614,7 +648,13 @@
         + jnp.roll(kv_lin, -(ROT // 2), 1) * back_key
         + jnp.roll(kv_lin, ROT // 2, 1) * ahead_key
     ).astype(BF)
-    kv_all = relative(jnp.concatenate(tp_gather(key_cache, 0), axis=0), 0, "tp")
+    gathered = tp_gather(jnp.concatenate([key_cache, shift_own], axis=0), 0)
+    kv_all = relative(jnp.concatenate([g[:rows] for g in gathered], axis=0), 0, "tp")
+    shifts = jnp.concatenate(
+        [g[rows:].reshape(1, -1)[:, :shift_size] for g in gathered], axis=0
+    ).astype(F32)
+    query_shift = shifts[:, :heads_tp].reshape(-1)
+    up_shift = shifts[::2, heads_tp:].reshape(1, -1)
 
     query_lin = dot(low_one, query_mat, 1, 0) + query_shift
     grad_attended = dot(cotangent, out_mat, 1, 0).astype(BF)
@@ -658,8 +698,8 @@
     )
     part_kept, part_sent, ffn_vectors, up_kept, down_kept = ffn_out[:5]
     up_sent, down_sent = ffn_out[5:] if blocks > 1 else (None, None)
-    part = part_kept.astype(F32) + swap_fsdp(part_sent, 1).astype(F32)
-    part_tp = swap_tp(part[:, 2:].astype(BF), 1)
+    part_core = swap_fsdp(part_sent, 1)
+    part_tp = swap_tp(add_low(part_kept[:, 2:], part_core[:, 2:]), 1)
     up_sum = chip_scatter(up_kept, up_sent, (2, 4))
     down_sum = chip_scatter(down_kept, down_sent, (4, 2))
     ffn_sum = tp_scatter_even(jnp.concatenate([up_sum, down_sum], axis=1), hidden_half)
@@ -670,7 +710,7 @@
     up_shift_grad = ffn_vectors[2, :hidden_own].reshape(-1, hidden_half)
 
     attended_out = dot(attended, out_mat, 1, 1)
-    kv_pieces = relative(kv_grad, 0, "tp").reshape(tp_count, rows, -1)
+    kv_pieces = relative(kv_grad.T, 0, "tp").reshape(tp_count, rows, -1)
     kv_sum = tp_scatter([kv_pieces[r] for r in range(tp_count)], 0)
     kv_low_grad = (
         kv_sum * cos_key
@@ -739,22 +779,10 @@
         vectors = vectors[:half] + swap_fsdp(vectors[half:], bit)
     for bit in bits_of(tp_count):
         vectors = vectors + swap_tp(vectors, bit)
-    part_tp, vectors = lax.optimization_barrier((part_tp, vectors))
-    part = part[:, :2] + part_tp.astype(F32)
-    branch = part[0].reshape(rows, width)
-    norm_two_grad = part[1].reshape(rows, width)
-    output = (inputs + attended_out + out_shift + branch + down_shift).astype(BF)
-    scaled = norm_one_grad * gain_one + norm_two_grad * gain_two
-    input_grad = (
-        cotangent.astype(F32)
-        + inverse
-        * (
-            scaled
-            - jnp.mean(scaled, axis=-1, keepdims=True)
-            - normal * jnp.mean(scaled * normal, axis=-1, keepdims=True)
-        )
-    ).astype(BF)
-
+    output, input_grad = finish(
+        *(part_kept, part_core, part_tp, tokens, cotangent, attended_out),
+        *(norm_one_grad, gain_one, gain_two, out_shift + down_shift),
+    )
     vectors = vectors[0]
     features = vectors[shard : shard + 5, :shard]
     tail = vectors[shard + 5 :]

time: 285 us -> 274 us (0.961)
  waiting for transfers between devices: 99.1 us -> 90.4 us
  other arithmetic: 25 us -> 21 us
  local copies, waits for them, and re-layouts: 16.3 us -> 19.7 us
    ppermute x47 -> x45, waiting for transfers between devices: 99.1 us -> 90.4 us  [swap(): return lax.ppermute(value, axis, [(i, i ^ bit) for i in range(count)])]
    pallas_call x2, Pallas kernels: 50.1 us -> 44.4 us  [attention(): pl.pallas_call(lambda *refs: attention_kernel(first, *refs), out_shape=(j...]
    pallas_call x0 -> x1, Pallas kernels: none -> 5.01 us  [finish(): call(kept, taken, from_pair, tokens, grad, base, one_grad, gain_one, gain...]
    ppermute x47 -> x45, starting transfers between devices: 48.1 us -> 46.2 us  [swap(): return lax.ppermute(value, axis, [(i, i ^ bit) for i in range(count)])]
    unnamed x50 -> x78, local copies, waits for them, and re-layouts: 6.02 us -> 5.46 us
  transfers between devices with their start and end apart: 47 -> 45, of which waited for: 28 -> 24; matrix products, arithmetic and copies ran while one was open for 12% -> 17% of each run, Pallas kernels for 28% -> 19%
where the time goes in v1:
time: 274 us; the launch traced here: 273 us
  waiting for transfers between devices  90.4 us (33%)
  Pallas kernels  81.8 us (30%)
  starting transfers between devices  46.2 us (17%)
  other arithmetic  21 us (8%)
  local copies, waits for them, and re-layouts  19.7 us (7%)
  matrix products  12.1 us (4%)
    ppermute x45, waiting for transfers between devices, swap(): return lax.ppermute(value, axis, [(i, i ^ bit) for i in range(count)])  90.4 us
    ppermute x45, starting transfers between devices, swap(): return lax.ppermute(value, axis, [(i, i ^ bit) for i in range(count)])  46.2 us
    pallas_call x2, Pallas kernels, attention(): pl.pallas_call(lambda *refs: attention_kernel(first, *refs), out_shape=(j...  44.4 us
    pallas_call x4, Pallas kernels, local_kernel(): pl.pallas_call(kernel, out_shape=[jax.ShapeDtypeStruct(shape, kind) for s...  32.4 us
    dot_general x7, matrix products, dot(): lax.dot_general(left, right, (((left_dim,), (right_dim,)), ((), ())), pre...  11.8 us
  transfers between devices with their start and end apart: 45, of which 24 were waited for; matrix products, arithmetic and copies ran while one was open for 17% of the time, Pallas kernels for 19%

profile of v1, /device:TPU:0, one launch (start us, length us, event | category | flops | bytes accessed | tf_op | source)
XLA Modules:
  0.0 273.1 jit_solution(1942016737108629035)
XLA Ops:
  1.3 2.0 shard_map.305
  7.0 1.5 fusion.7
  9.4 2.6 collective-permute-start.1
  12.1 2.5 collective-permute-done.1
  14.6 1.8 collective-permute-start.2
  17.4 2.6 collective-permute-start.6
  25.0 1.6 collective-permute-start.7
  28.2 2.3 collective-permute-start.3
  30.8 2.5 collective-permute-start.10
  35.7 5.9 %collective-permute-done.10.refs_3_ = bf16[192,768]{1,0:T(8,128)(2,1)S(1)} collective-permute-done((bf16[192,768]{1,0:T(8,128)(2,1)S(1)}, bf16[192,768]{1,0:T(8,128)(2,1)S(1)}, u32[]{:S(2)}, u32[]{:S(2)}) %collective-permute-start.10) | collective-permute-done | bytes 294944 | tf_op jit(solution)/shard_map/ppermute | solution.py:36
  41.7 3.9 %collective-permute-done.9.refs_2_ = bf16[192,768]{1,0:T(8,128)(2,1)S(1)} collective-permute-done((bf16[192,768]{1,0:T(8,128)(2,1)S(1)}, bf16[192,768]{1,0:T(8,128)(2,1)S(1)}, u32[]{:S(2)}, u32[]{:S(2)}) %collective-permute-start.9) | collective-permute-done | bytes 294944 | tf_op jit(solution)/shard_map/ppermute | solution.py:36
  47.5 2.4 shard_map.306
  49.8 1.7 fusion.66
  51.6 1.7 collective-permute-start.12
  56.1 5.4 %collective-permute-done.18 = bf16[192,768]{1,0:T(8,128)(2,1)} collective-permute-done((bf16[192,768]{1,0:T(8,128)(2,1)}, bf16[192,768]{1,0:T(8,128)(2,1)}, u32[]{:S(2)}, u32[]{:S(2)}) %collective-permute-start.18) | collective-permute-done | bytes 294944 | tf_op jit(solution)/shard_map/ppermute | solution.py:36
  61.5 1.7 fusion.67
  63.3 2.0 fusion.8.refs_2_
  66.1 31.4 %shard_map.307 = (bf16[448,768]{1,0:T(8,128)(2,1)S(1)}, bf16[448,768]{1,0:T(8,128)(2,1)S(1)}, f32[128,1792]{1,0:T(8,128)S(1)}) custom-call(s32[7,3]{1,0:T(8,128)S(1)} %pad_add_fusion.refs_0_, f32[448,768]{1,0:T(8,128)S(1)} %convolution_add_fusion.1.refs_1_, bf16[448,768]{1,0:T(8,128)(2,1)S(1)} %fusion.8.refs_2_, ...), custom_call_target="tpu_custom_call" | custom-call | flops 15099494400 | bytes 688128 | tf_op jit(solution)/shard_map/pallas_call | solution.py:287
  97.5 13.0 %shard_map.308 = (bf16[448,768]{1,0:T(8,128)(2,1)S(1)}, bf16[448,768]{1,0:T(8,128)(2,1)S(1)}, f32[128,1792]{1,0:T(8,128)S(1)}) custom-call(s32[7,3]{1,0:T(8,128)S(1)} %pad_add_fusion.refs_0_, f32[448,768]{1,0:T(8,128)S(1)} %convolution_add_fusion.1.refs_1_, bf16[448,768]{1,0:T(8,128)(2,1)S(1)} %fusion.8.refs_2_, ...), custom_call_target="tpu_custom_call", output_to_operand_aliasing={{0}: (7, {}), {1}: (8, {})} | custom-call | flops 6039797760 | bytes 688128 | tf_op jit(solution)/shard_map/pallas_call | solution.py:287
  111.4 2.0 collective-permute-start.24
  113.4 1.9 pad_maximum_fusion.refs_12_
  115.2 2.0 collective-permute-start.21
  117.3 1.6 collective-permute-done.24
  120.1 6.4 %collective-permute-done.25 = bf16[448,128]{1,0:T(8,128)(2,1)S(1)} collective-permute-done((bf16[448,128]{1,0:T(8,128)(2,1)S(1)}, bf16[448,128]{1,0:T(8,128)(2,1)S(1)}, u32[]{:S(2)}, u32[]{:S(2)}) %collective-permute-start.25) | collective-permute-done | bytes 114720 | tf_op jit(solution)/shard_map/ppermute | solution.py:36
  126.8 1.4 convert_reduce_fusion.3
  130.4 2.1 collective-permute-start.19
  132.5 3.5 %fusion.6 = (f32[768]{0:T(1024)S(1)}, f32[768]{0:T(1024)S(1)}, f32[448,768]{1,0:T(8,128)}) fusion(bf16[448,768]{1,0:T(8,128)(2,1)} %tokens.1, f32[448]{0:T(512)S(1)} %add_rsqrt_fusion, f32[448]{0:T(512)S(1)} %broadcast_multiply_fusion, f32[448,768]{1,0:T(8,128)} %fusion.75, bf16[448,768]{1,0:T(8,128)(2,1)S(1)} %get-tuple-element.72.query_low, ...), kind=kOutput, calls=%fused_computation.12 | convolution fusion | flops 531479040 | bytes 6497793 | tf_op jit(solution)/shard_map/dot_general | solution.py:25
  136.6 9.4 %collective-permute-done.20.refs_14_ = bf16[192,1536]{1,0:T(8,128)(2,1)} collective-permute-done((bf16[192,1536]{1,0:T(8,128)(2,1)}, bf16[192,1536]{1,0:T(8,128)(2,1)}, u32[]{:S(2)}, u32[]{:S(2)}) %collective-permute-start.20) | collective-permute-done | bytes 589856 | tf_op jit(solution)/shard_map/ppermute | solution.py:36
  146.5 23.2 %shard_map.309 = (bf16[2,4,224,768]{3,2,1,0:T(8,128)(2,1)}, bf16[2,4,224,768]{3,2,1,0:T(8,128)(2,1)}, f32[8,768]{1,0:T(8,128)}, bf16[2,192,768]{2,1,0:T(8,128)(2...) custom-call(s32[2]{0:T(128)} %pad_add_fusion.1.place.refs_0_, ...), custom_call_target="tpu_custom_call" | custom-call | flops 12683575296 | bytes 1048576 | tf_op jit(solution)/shard_map/pallas_call | solution.py:319
  172.7 4.8 %shard_map.310 = (bf16[4,192,768]{2,1,0:T(8,128)(2,1)}, bf16[4,192,768]{2,1,0:T(8,128)(2,1)}) custom-call(s32[2]{0:T(128)} %pad_add_fusion.1.place.refs_0_, bf16[448,768]{1,0:T(8,128)(2,1)} %copy-done.5, bf16[448,768]{1,0:T(8,128)(2,1)} %copy-done.2, bf16[448,768]{1,0:T(8,128)(2,1)} %grad.3, bf16[448,768]{1,0:T(8,128)(2,1)} %copy-done), custom_call_target="tpu_custom_call" | custom-call | flops 1056964608 | bytes 1048576 | tf_op jit(solution)/shard_map/pallas_call | solution.py:319
  179.3 3.9 %collective-permute-done.27 = f32[2,110,128]{2,1,0:T(8,128)S(1)} collective-permute-done((f32[2,110,128]{2,1,0:T(8,128)S(1)}, f32[2,110,128]{2,1,0:T(8,128)S(1)}, u32[]{:S(2)}, u32[]{:S(2)}) %collective-permute-start.27) | collective-permute-done | bytes 112672 | tf_op jit(solution)/shard_map/ppermute | solution.py:36
  183.3 1.8 collective-permute-start.28
  187.6 3.4 %fusion.12.base = f32[448,768]{1,0:T(8,128)} fusion(bf16[448,768]{1,0:T(8,128)(2,1)S(1)} %copy-done.1, bf16[768,768]{1,0:T(8,128)(2,1)} %collective-permute-done.11, bf16[768,768]{1,0:T(8,128)(2,1)S(1)} %copy-done.8, pred[]{:T(512)S(6)} %eq.25), kind=kOutput, calls=%fused_computation.34 | convolution fusion | flops 529072128 | bytes 4423681 | tf_op jit(solution)/shard_map/dot_general | solution.py:25
  191.0 1.7 collective-permute-start.39
  193.2 1.6 collective-permute-start.30
  194.9 1.6 add_convert_fusion.1
  198.5 1.6 collective-permute-start.34
  202.3 4.5 %collective-permute-done.39 = bf16[2,192,768]{2,1,0:T(8,128)(2,1)S(1)} collective-permute-done((bf16[2,192,768]{2,1,0:T(8,128)(2,1)}, bf16[2,192,768]{2,1,0:T(8,128)(2,1)S(1)}, u32[]{:S(2)}, u32[]{:S(2)}) %collective-permute-start.39) | collective-permute-done | bytes 589856 | tf_op jit(solution)/shard_map/ppermute | solution.py:36
  208.0 1.7 collective-permute-start.42
  209.7 3.3 %collective-permute-done.32 = bf16[2,192,384]{2,1,0:T(8,128)(2,1)S(1)} collective-permute-done((bf16[2,192,384]{2,1,0:T(8,128)(2,1)S(1)}, bf16[2,192,384]{2,1,0:T(8,128)(2,1)S(1)}, u32[]{:S(2)}, u32[]{:S(2)}) %collective-permute-start.32) | collective-permute-done | bytes 294944 | tf_op jit(solution)/shard_map/ppermute | solution.py:36
  215.7 2.8 %collective-permute-done.40 = bf16[1,192,768]{2,1,0:T(8,128)(2,1)S(1)} collective-permute-done((bf16[1,192,768]{2,1,0:T(8,128)(2,1)S(1)}, bf16[1,192,768]{2,1,0:T(8,128)(2,1)S(1)}, u32[]{:S(2)}, u32[]{:S(2)}) %collective-permute-start.40) | collective-permute-done | bytes 294944 | tf_op jit(solution)/shard_map/ppermute | solution.py:36
  221.1 1.9 collective-permute-start.36
  223.1 5.2 %collective-permute-done.36 = bf16[192,384]{1,0:T(8,128)(2,1)S(1)} collective-permute-done((bf16[192,384]{1,0:T(8,128)(2,1)S(1)}, bf16[192,384]{1,0:T(8,128)(2,1)S(1)}, u32[]{:S(2)}, u32[]{:S(2)}) %collective-permute-start.36) | collective-permute-done | bytes 147488 | tf_op jit(solution)/shard_map/ppermute | solution.py:36
  229.7 1.9 collective-permute-start.43
  231.6 3.8 %collective-permute-done.37 = bf16[192,192]{1,0:T(8,128)(2,1)S(1)} collective-permute-done((bf16[192,192]{1,0:T(8,128)(2,1)S(1)}, bf16[192,192]{1,0:T(8,128)(2,1)S(1)}, u32[]{:S(2)}, u32[]{:S(2)}) %collective-permute-start.37) | collective-permute-done | bytes 73760 | tf_op jit(solution)/shard_map/ppermute | solution.py:36
  238.2 3.5 %collective-permute-done.43 = bf16[192,768]{1,0:T(8,128)(2,1)S(1)} collective-permute-done((bf16[192,768]{1,0:T(8,128)(2,1)S(1)}, bf16[192,768]{1,0:T(8,128)(2,1)S(1)}, u32[]{:S(2)}, u32[]{:S(2)}) %collective-permute-start.43) | collective-permute-done | bytes 294944 | tf_op jit(solution)/shard_map/ppermute | solution.py:36
  245.9 20.6 %collective-permute-done.23.from_pair = bf16[2,2,224,768]{3,2,1,0:T(8,128)(2,1)S(1)} collective-permute-done((bf16[2,2,224,768]{3,2,1,0:T(8,128)(2,1)S(1)}, bf16[2,2,224,768]{3,2,1,0:T(8,128)(2,1)S(1)}, u32[]{:S(2)}, u32[]{:S(2)}) %collective-permute-start.23) | collective-permute-done | bytes 1376288 | tf_op jit(solution)/shard_map/ppermute | solution.py:36
  267.6 5.0 %finish.1 = (bf16[448,768]{1,0:T(8,128)(2,1)}, bf16[448,768]{1,0:T(8,128)(2,1)}) custom-call(bf16[2,4,224,768]{3,2,1,0:T(8,128)(2,1)} %get-tuple-element.69.kept, bf16[2,4,224,768]{3,2,1,0:T(8,128)(2,1)} %copy-done.4, bf16[2,2,224,768]{3,2,1,0:T(8,128)(2,1)} %copy-done.13, bf16[448,768]{1,0:T(8,128)(2,1)} %tokens.1, bf16[448,768]{1,0:T(8,128)(2,1)} %grad.3, ...), custom_call_target="tpu_custom_call" | custom-call | flops 10321920 | bytes 8257536 | tf_op jit(solution)/shard_map/finish/pallas_call | solution.py:431
  (286 shorter events, 54.5 us)
Async XLA Ops:
  3.3 6.1 %collective-permute-start = (bf16[1,112,128]{2,1,0:T(8,128)(2,1)}, bf16[1,112,128]{2,1,0:T(8,128)(2,1)S(1)}, u32[]{:S(2)}, u32[]{:S(2)}) collective-permute-start(bf16[1,112,128]{2,1,0:T(8,128)(2,1)} %bitcast.119), channel_id=1, source_target_pairs={{0,4},{4,0},{8,12},{12,8},{16,20},{20,16},{24,28},{28,24},{1,5},{5... | collective-permute-start | bytes 86024 | tf_op jit(solution)/shard_map/ppermute | solution.py:36
  3.9 12.5 %collective-permute-start.5 = (bf16[96,960]{1,0:T(8,128)(2,1)}, bf16[96,960]{1,0:T(8,128)(2,1)S(1)}, u32[]{:S(2)}, u32[]{:S(2)}) collective-permute-start(bf16[96,960]{1,0:T(8,128)(2,1)} %get-tuple-element.52), channel_id=1, source_target_pairs={{0,4},{4,0},{8,12},{12,8},{16,20},{20,16},{24,28},{28,24},{1,5},{5... | collective-permute-start | bytes 552968 | tf_op jit(solution)/shard_map/ppermute | solution.py:36
  4.0 125.8 %collective-permute-start.16 = (bf16[448,768]{1,0:T(8,128)(2,1)}, bf16[448,768]{1,0:T(8,128)(2,1)}, u32[]{:S(2)}, u32[]{:S(2)}) collective-permute-start(bf16[448,768]{1,0:T(8,128)(2,1)} %grad.3), channel_id=1, source_target_pairs={{0,4},{4,0},{8,12},{12,8},{16,20},{20,16},{24,28},{28,24},{1,5},{5... | collective-permute-start | bytes 2064392 | tf_op jit(solution)/shard_map/ppermute | solution.py:36
  9.4 5.1 %collective-permute-start.1 = (bf16[2,112,128]{2,1,0:T(8,128)(2,1)S(1)}, bf16[2,112,128]{2,1,0:T(8,128)(2,1)S(1)}, u32[]{:S(2)}, u32[]{:S(2)}) collective-permute-start(bf16[2,112,128]{2,1,0:T(8,128)(2,1)S(1)} %maximum_select_fusion.3), channel_id=1, source_target_pairs={{0,8},{4,12},{8,0},{12,4},{16,24},{20,28},{24,16},{28,20},{1,9},{5... | collective-permute-start | bytes 172040 | tf_op jit(solution)/shard_map/ppermute | solution.py:36
  14.6 5.4 %collective-permute-start.2 = (bf16[4,112,128]{2,1,0:T(8,128)(2,1)S(1)}, bf16[4,112,128]{2,1,0:T(8,128)(2,1)S(1)}, u32[]{:S(2)}, u32[]{:S(2)}) collective-permute-start(bf16[4,112,128]{2,1,0:T(8,128)(2,1)S(1)} %pad_maximum_fusion.12), channel_id=1, source_target_pairs={{0,16},{4,20},{8,24},{12,28},{16,0},{20,4},{24,8},{28,12},{1,17},{... | collective-permute-start | bytes 344072 | tf_op jit(solution)/shard_map/ppermute | solution.py:36
  17.4 7.5 %collective-permute-start.6 = (bf16[192,192]{1,0:T(8,128)(2,1)S(1)}, bf16[192,192]{1,0:T(8,128)(2,1)S(1)}, u32[]{:S(2)}, u32[]{:S(2)}) collective-permute-start(bf16[192,192]{1,0:T(8,128)(2,1)S(1)} %slice.518), channel_id=1, source_target_pairs={{0,2},{1,3},{2,0},{3,1},{4,6},{5,7},{6,4},{7,5},{8,10},{9,11},{10,... | collective-permute-start | bytes 221192 | tf_op jit(solution)/shard_map/ppermute | solution.py:36
  22.8 42.5 %copy-start.5 = (bf16[448,768]{1,0:T(8,128)(2,1)}, bf16[448,768]{1,0:T(8,128)(2,1)S(1)}, u32[]{:S(2)}) copy-start(bf16[448,768]{1,0:T(8,128)(2,1)S(1)} %fusion.5.one) | copy-start | bytes 2064388
  24.9 28.5 %copy-start.10 = (bf16[448,128]{1,0:T(8,128)(2,1)}, bf16[448,128]{1,0:T(8,128)(2,1)S(1)}, u32[]{:S(2)}) copy-start(bf16[448,128]{1,0:T(8,128)(2,1)S(1)} %get-tuple-element.253) | copy-start | bytes 344068
  25.0 5.5 %collective-permute-start.7 = (bf16[192,384]{1,0:T(8,128)(2,1)S(1)}, bf16[192,384]{1,0:T(8,128)(2,1)S(1)}, u32[]{:S(2)}, u32[]{:S(2)}) collective-permute-start(bf16[192,384]{1,0:T(8,128)(2,1)S(1)} %pad_maximum_fusion.9), channel_id=1, source_target_pairs={{0,1},{1,0},{2,3},{3,2},{4,5},{5,4},{6,7},{7,6},{8,9},{9,8},{10,11... | collective-permute-start | bytes 442376 | tf_op jit(solution)/shard_map/ppermute | solution.py:36
  28.2 7.3 %collective-permute-start.3 = (bf16[464,128]{1,0:T(8,128)(2,1)S(1)}, bf16[464,128]{1,0:T(8,128)(2,1)S(1)}, u32[]{:S(2)}, u32[]{:S(2)}) collective-permute-start(bf16[464,128]{1,0:T(8,128)(2,1)S(1)} %pad_maximum_fusion.11), channel_id=1, source_target_pairs={{0,2},{1,3},{2,0},{3,1},{4,6},{5,7},{6,4},{7,5},{8,10},{9,11},{10,... | collective-permute-start | bytes 356360 | tf_op jit(solution)/shard_map/ppermute | solution.py:36
  30.8 10.9 %collective-permute-start.10 = (bf16[192,768]{1,0:T(8,128)(2,1)S(1)}, bf16[192,768]{1,0:T(8,128)(2,1)S(1)}, u32[]{:S(2)}, u32[]{:S(2)}) collective-permute-start(bf16[192,768]{1,0:T(8,128)(2,1)S(1)} %pad_maximum_fusion.4.refs_0_), channel_id=1, source_target_pairs={{0,24},{4,28},{8,16},{12,20},{16,8},{20,12},{24,0},{28,4},{1,25},{... | collective-permute-start | bytes 884744 | tf_op jit(solution)/shard_map/ppermute | solution.py:36
  33.3 12.2 %collective-permute-start.9 = (bf16[192,768]{1,0:T(8,128)(2,1)S(1)}, bf16[192,768]{1,0:T(8,128)(2,1)S(1)}, u32[]{:S(2)}, u32[]{:S(2)}) collective-permute-start(bf16[192,768]{1,0:T(8,128)(2,1)S(1)} %pad_maximum_fusion.4.refs_0_), channel_id=1, source_target_pairs={{0,16},{4,20},{8,24},{12,28},{16,0},{20,4},{24,8},{28,12},{1,17},{... | collective-permute-start | bytes 884744 | tf_op jit(solution)/shard_map/ppermute | solution.py:36
  33.8 12.9 %collective-permute-start.8 = (bf16[192,768]{1,0:T(8,128)(2,1)S(1)}, bf16[192,768]{1,0:T(8,128)(2,1)S(1)}, u32[]{:S(2)}, u32[]{:S(2)}) collective-permute-start(bf16[192,768]{1,0:T(8,128)(2,1)S(1)} %pad_maximum_fusion.4.refs_0_), channel_id=1, source_target_pairs={{0,8},{4,12},{8,0},{12,4},{16,24},{20,28},{24,16},{28,20},{1,9},{5... | collective-permute-start | bytes 884744 | tf_op jit(solution)/shard_map/ppermute | solution.py:36
  35.5 16.0 %collective-permute-start.4 = (bf16[928,128]{1,0:T(8,128)(2,1)S(1)}, bf16[928,128]{1,0:T(8,128)(2,1)S(1)}, u32[]{:S(2)}, u32[]{:S(2)}) collective-permute-start(bf16[928,128]{1,0:T(8,128)(2,1)S(1)} %pad_maximum_fusion.6), channel_id=1, source_target_pairs={{0,1},{1,0},{2,3},{3,2},{4,5},{5,4},{6,7},{7,6},{8,9},{9,8},{10,11... | collective-permute-start | bytes 712712 | tf_op jit(solution)/shard_map/ppermute | solution.py:36
  41.7 88.7 %collective-permute-start.14 = (bf16[448,768]{1,0:T(8,128)(2,1)}, bf16[448,768]{1,0:T(8,128)(2,1)}, u32[]{:S(2)}, u32[]{:S(2)}) collective-permute-start(bf16[448,768]{1,0:T(8,128)(2,1)} %tokens.1), channel_id=1, source_target_pairs={{0,4},{4,0},{8,12},{12,8},{16,20},{20,16},{24,28},{28,24},{1,5},{5... | collective-permute-start | bytes 2064392 | tf_op jit(solution)/shard_map/ppermute | solution.py:36
  45.5 16.0 %collective-permute-start.18 = (bf16[192,768]{1,0:T(8,128)(2,1)}, bf16[192,768]{1,0:T(8,128)(2,1)}, u32[]{:S(2)}, u32[]{:S(2)}) collective-permute-start(bf16[192,768]{1,0:T(8,128)(2,1)} %slice.525), channel_id=1, source_target_pairs={{0,2},{1,3},{2,0},{3,1},{4,6},{5,7},{6,4},{7,5},{8,10},{9,11},{10,... | collective-permute-start | bytes 884744 | tf_op jit(solution)/shard_map/ppermute | solution.py:36
  49.8 13.4 %collective-permute-start.11 = (bf16[768,768]{1,0:T(8,128)(2,1)}, bf16[768,768]{1,0:T(8,128)(2,1)}, u32[]{:S(2)}, u32[]{:S(2)}) collective-permute-start(bf16[768,768]{1,0:T(8,128)(2,1)} %shard_map.306), channel_id=1, source_target_pairs={{0,4},{4,0},{8,12},{12,8},{16,20},{20,16},{24,28},{28,24},{1,5},{5... | collective-permute-start | bytes 3538952 | tf_op jit(solution)/shard_map/ppermute | solution.py:36
  51.6 45.9 %collective-permute-start.12 = (bf16[448,768]{1,0:T(8,128)(2,1)}, bf16[448,768]{1,0:T(8,128)(2,1)}, u32[]{:S(2)}, u32[]{:S(2)}) collective-permute-start(bf16[448,768]{1,0:T(8,128)(2,1)} %tokens.1), channel_id=1, source_target_pairs={{0,1},{1,0},{2,3},{3,2},{4,5},{5,4},{6,7},{7,6},{8,9},{9,8},{10,11... | collective-permute-start | bytes 2064392 | tf_op jit(solution)/shard_map/ppermute | solution.py:36
  61.5 35.9 %collective-permute-start.13 = (bf16[448,768]{1,0:T(8,128)(2,1)S(1)}, bf16[448,768]{1,0:T(8,128)(2,1)S(1)}, u32[]{:S(2)}, u32[]{:S(2)}) collective-permute-start(bf16[448,768]{1,0:T(8,128)(2,1)S(1)} %copy-done.9), channel_id=1, source_target_pairs={{0,1},{1,0},{2,3},{3,2},{4,5},{5,4},{6,7},{7,6},{8,9},{9,8},{10,11... | collective-permute-start | bytes 2064392 | tf_op jit(solution)/shard_map/ppermute | solution.py:36
  111.4 7.4 %collective-permute-start.24 = (bf16[896,128]{1,0:T(8,128)(2,1)S(1)}, bf16[896,128]{1,0:T(8,128)(2,1)S(1)}, u32[]{:S(2)}, u32[]{:S(2)}) collective-permute-start(bf16[896,128]{1,0:T(8,128)(2,1)S(1)} %pad_maximum_fusion.8), channel_id=1, source_target_pairs={{0,1},{1,0},{2,3},{3,2},{4,5},{5,4},{6,7},{7,6},{8,9},{9,8},{10,11... | collective-permute-start | bytes 688136 | tf_op jit(solution)/shard_map/ppermute | solution.py:36
  115.2 21.3 %collective-permute-start.21 = (bf16[192,1536]{1,0:T(8,128)(2,1)}, bf16[192,1536]{1,0:T(8,128)(2,1)}, u32[]{:S(2)}, u32[]{:S(2)}) collective-permute-start(bf16[192,1536]{1,0:T(8,128)(2,1)} %pad_maximum_fusion.refs_12_), channel_id=1, source_target_pairs={{0,24},{4,28},{8,16},{12,20},{16,8},{20,12},{24,0},{28,4},{1,25},{... | collective-permute-start | bytes 1769480 | tf_op jit(solution)/shard_map/ppermute | solution.py:36
  118.9 7.6 %collective-permute-start.25 = (bf16[448,128]{1,0:T(8,128)(2,1)S(1)}, bf16[448,128]{1,0:T(8,128)(2,1)S(1)}, u32[]{:S(2)}, u32[]{:S(2)}) collective-permute-start(bf16[448,128]{1,0:T(8,128)(2,1)S(1)} %fusion.21), channel_id=1, source_target_pairs={{0,2},{1,3},{2,0},{3,1},{4,6},{5,7},{6,4},{7,5},{8,10},{9,11},{10,... | collective-permute-start | bytes 344072 | tf_op jit(solution)/shard_map/ppermute | solution.py:36
  120.1 26.5 %collective-permute-start.15 = (bf16[448,768]{1,0:T(8,128)(2,1)}, bf16[448,768]{1,0:T(8,128)(2,1)}, u32[]{:S(2)}, u32[]{:S(2)}) collective-permute-start(bf16[448,768]{1,0:T(8,128)(2,1)} %collective-permute-done.12.refs_5_), channel_id=1, source_target_pairs={{0,4},{4,0},{8,12},{12,8},{16,20},{20,16},{24,28},{28,24},{1,5},{5... | collective-permute-start | bytes 2064392 | tf_op jit(solution)/shard_map/ppermute | solution.py:36
  126.5 20.1 %collective-permute-start.17 = (bf16[448,768]{1,0:T(8,128)(2,1)}, bf16[448,768]{1,0:T(8,128)(2,1)}, u32[]{:S(2)}, u32[]{:S(2)}) collective-permute-start(bf16[448,768]{1,0:T(8,128)(2,1)} %copy-done.30), channel_id=1, source_target_pairs={{0,4},{4,0},{8,12},{12,8},{16,20},{20,16},{24,28},{28,24},{1,5},{5... | collective-permute-start | bytes 2064392 | tf_op jit(solution)/shard_map/ppermute | solution.py:36
  129.8 16.1 %collective-permute-start.20 = (bf16[192,1536]{1,0:T(8,128)(2,1)}, bf16[192,1536]{1,0:T(8,128)(2,1)}, u32[]{:S(2)}, u32[]{:S(2)}) collective-permute-start(bf16[192,1536]{1,0:T(8,128)(2,1)} %pad_maximum_fusion.refs_12_), channel_id=1, source_target_pairs={{0,16},{4,20},{8,24},{12,28},{16,0},{20,4},{24,8},{28,12},{1,17},{... | collective-permute-start | bytes 1769480 | tf_op jit(solution)/shard_map/ppermute | solution.py:36
  130.4 16.2 %collective-permute-start.19 = (bf16[192,1536]{1,0:T(8,128)(2,1)}, bf16[192,1536]{1,0:T(8,128)(2,1)}, u32[]{:S(2)}, u32[]{:S(2)}) collective-permute-start(bf16[192,1536]{1,0:T(8,128)(2,1)} %pad_maximum_fusion.refs_12_), channel_id=1, source_target_pairs={{0,8},{4,12},{8,0},{12,4},{16,24},{20,28},{24,16},{28,20},{1,9},{5... | collective-permute-start | bytes 1769480 | tf_op jit(solution)/shard_map/ppermute | solution.py:36
  172.6 5.4 %collective-permute-start.26 = (f32[4,110,128]{2,1,0:T(8,128)S(1)}, f32[4,110,128]{2,1,0:T(8,128)S(1)}, u32[]{:S(2)}, u32[]{:S(2)}) collective-permute-start(f32[4,110,128]{2,1,0:T(8,128)S(1)} %select_bitcast_fusion), channel_id=1, source_target_pairs={{0,4},{4,0},{8,12},{12,8},{16,20},{20,16},{24,28},{28,24},{1,5},{5... | collective-permute-start | bytes 675848 | tf_op jit(solution)/shard_map/ppermute | solution.py:36
  177.5 17.3 %collective-permute-start.31 = (bf16[4,192,768]{2,1,0:T(8,128)(2,1)}, bf16[4,192,768]{2,1,0:T(8,128)(2,1)}, u32[]{:S(2)}, u32[]{:S(2)}) collective-permute-start(bf16[4,192,768]{2,1,0:T(8,128)(2,1)} %get-tuple-element.78), channel_id=1, source_target_pairs={{0,4},{4,0},{8,12},{12,8},{16,20},{20,16},{24,28},{28,24},{1,5},{5... | collective-permute-start | bytes 3538952 | tf_op jit(solution)/shard_map/ppermute | solution.py:36
  178.1 5.1 %collective-permute-start.27 = (f32[2,110,128]{2,1,0:T(8,128)S(1)}, f32[2,110,128]{2,1,0:T(8,128)S(1)}, u32[]{:S(2)}, u32[]{:S(2)}) collective-permute-start(f32[2,110,128]{2,1,0:T(8,128)S(1)} %slice.554), channel_id=1, source_target_pairs={{0,16},{4,20},{8,24},{12,28},{16,0},{20,4},{24,8},{28,12},{1,17},{... | collective-permute-start | bytes 337928 | tf_op jit(solution)/shard_map/ppermute | solution.py:36
  183.3 4.2 %collective-permute-start.28 = (f32[1,110,128]{2,1,0:T(8,128)S(1)}, f32[1,110,128]{2,1,0:T(8,128)S(1)}, u32[]{:S(2)}, u32[]{:S(2)}) collective-permute-start(f32[1,110,128]{2,1,0:T(8,128)S(1)} %slice.556), channel_id=1, source_target_pairs={{0,8},{4,12},{8,0},{12,4},{16,24},{20,28},{24,16},{28,20},{1,9},{5... | collective-permute-start | bytes 168968 | tf_op jit(solution)/shard_map/ppermute | solution.py:36
  187.5 5.7 %collective-permute-start.29 = (f32[1,110,128]{2,1,0:T(8,128)S(1)}, f32[1,110,128]{2,1,0:T(8,128)S(1)}, u32[]{:S(2)}, u32[]{:S(2)}) collective-permute-start(f32[1,110,128]{2,1,0:T(8,128)S(1)} %slice_add_fusion.5), channel_id=1, source_target_pairs={{0,1},{1,0},{2,3},{3,2},{4,5},{5,4},{6,7},{7,6},{8,9},{9,8},{10,11... | collective-permute-start | bytes 168968 | tf_op jit(solution)/shard_map/ppermute | solution.py:36
  191.0 15.7 %collective-permute-start.39 = (bf16[2,192,768]{2,1,0:T(8,128)(2,1)}, bf16[2,192,768]{2,1,0:T(8,128)(2,1)S(1)}, u32[]{:S(2)}, u32[]{:S(2)}) collective-permute-start(bf16[2,192,768]{2,1,0:T(8,128)(2,1)} %get-tuple-element.80), channel_id=1, source_target_pairs={{0,8},{4,12},{8,0},{12,4},{16,24},{20,28},{24,16},{28,20},{1,9},{5... | collective-permute-start | bytes 1769480 | tf_op jit(solution)/shard_map/ppermute | solution.py:36
  192.7 15.1 %collective-permute-start.41 = (bf16[2,192,768]{2,1,0:T(8,128)(2,1)S(1)}, bf16[2,192,768]{2,1,0:T(8,128)(2,1)S(1)}, u32[]{:S(2)}, u32[]{:S(2)}) collective-permute-start(bf16[2,192,768]{2,1,0:T(8,128)(2,1)S(1)} %copy-done.31), channel_id=1, source_target_pairs={{0,16},{4,20},{8,24},{12,28},{16,0},{20,4},{24,8},{28,12},{1,17},{... | collective-permute-start | bytes 1769480 | tf_op jit(solution)/shard_map/ppermute | solution.py:36
  193.2 42.3 %collective-permute-start.22 = (bf16[2,4,224,768]{3,2,1,0:T(8,128)(2,1)S(1)}, bf16[2,4,224,768]{3,2,1,0:T(8,128)(2,1)S(1)}, u32[]{:S(2)}, u32[]{:S(2)}) collective-permute-start(bf16[2,4,224,768]{3,2,1,0:T(8,128)(2,1)S(1)} %copy-done.29), channel_id=1, source_target_pairs={{0,4},{4,0},{8,12},{12,8},{16,20},{20,16},{24,28},{28,24},{1,5},{5... | collective-permute-start | bytes 8257544 | tf_op jit(solution)/shard_map/ppermute | solution.py:36
  193.2 5.3 %collective-permute-start.30 = (f32[1,110,128]{2,1,0:T(8,128)S(1)}, f32[1,110,128]{2,1,0:T(8,128)S(1)}, u32[]{:S(2)}, u32[]{:S(2)}) collective-permute-start(f32[1,110,128]{2,1,0:T(8,128)S(1)} %add.283), channel_id=1, source_target_pairs={{0,2},{1,3},{2,0},{3,1},{4,6},{5,7},{6,4},{7,5},{8,10},{9,11},{10,... | collective-permute-start | bytes 168968 | tf_op jit(solution)/shard_map/ppermute | solution.py:36
  196.6 16.4 %collective-permute-start.32 = (bf16[2,192,384]{2,1,0:T(8,128)(2,1)S(1)}, bf16[2,192,384]{2,1,0:T(8,128)(2,1)S(1)}, u32[]{:S(2)}, u32[]{:S(2)}) collective-permute-start(bf16[2,192,384]{2,1,0:T(8,128)(2,1)S(1)} %get-tuple-element.166), channel_id=1, source_target_pairs={{0,8},{4,12},{8,0},{12,4},{16,24},{20,28},{24,16},{28,20},{1,9},{5... | collective-permute-start | bytes 884744 | tf_op jit(solution)/shard_map/ppermute | solution.py:36
  198.5 15.6 %collective-permute-start.34 = (bf16[2,192,384]{2,1,0:T(8,128)(2,1)S(1)}, bf16[2,192,384]{2,1,0:T(8,128)(2,1)S(1)}, u32[]{:S(2)}, u32[]{:S(2)}) collective-permute-start(bf16[2,192,384]{2,1,0:T(8,128)(2,1)S(1)} %get-tuple-element.167), channel_id=1, source_target_pairs={{0,16},{4,20},{8,24},{12,28},{16,0},{20,4},{24,8},{28,12},{1,17},{... | collective-permute-start | bytes 884744 | tf_op jit(solution)/shard_map/ppermute | solution.py:36
  201.1 71.5 %copy-start.28 = (f32[96]{0:T(128)}, f32[96]{0:T(128)S(1)}, u32[]{:S(2)}) copy-start(f32[96]{0:T(128)S(1)} %get-tuple-element.268) | copy-start | bytes 1156
  206.9 11.6 %collective-permute-start.40 = (bf16[1,192,768]{2,1,0:T(8,128)(2,1)S(1)}, bf16[1,192,768]{2,1,0:T(8,128)(2,1)S(1)}, u32[]{:S(2)}, u32[]{:S(2)}) collective-permute-start(bf16[1,192,768]{2,1,0:T(8,128)(2,1)S(1)} %slice.580), channel_id=1, source_target_pairs={{0,16},{4,20},{8,24},{12,28},{16,0},{20,4},{24,8},{28,12},{1,17},{... | collective-permute-start | bytes 884744 | tf_op jit(solution)/shard_map/ppermute | solution.py:36
  208.0 15.1 %collective-permute-start.42 = (bf16[1,192,768]{2,1,0:T(8,128)(2,1)S(1)}, bf16[1,192,768]{2,1,0:T(8,128)(2,1)S(1)}, u32[]{:S(2)}, u32[]{:S(2)}) collective-permute-start(bf16[1,192,768]{2,1,0:T(8,128)(2,1)S(1)} %slice.584), channel_id=1, source_target_pairs={{0,8},{4,12},{8,0},{12,4},{16,24},{20,28},{24,16},{28,20},{1,9},{5... | collective-permute-start | bytes 884744 | tf_op jit(solution)/shard_map/ppermute | solution.py:36
  214.3 5.2 %collective-permute-start.35 = (bf16[1,192,384]{2,1,0:T(8,128)(2,1)S(1)}, bf16[1,192,384]{2,1,0:T(8,128)(2,1)S(1)}, u32[]{:S(2)}, u32[]{:S(2)}) collective-permute-start(bf16[1,192,384]{2,1,0:T(8,128)(2,1)S(1)} %slice.568), channel_id=1, source_target_pairs={{0,8},{4,12},{8,0},{12,4},{16,24},{20,28},{24,16},{28,20},{1,9},{5... | collective-permute-start | bytes 442376 | tf_op jit(solution)/shard_map/ppermute | solution.py:36
  215.7 5.1 %collective-permute-start.33 = (bf16[1,192,384]{2,1,0:T(8,128)(2,1)S(1)}, bf16[1,192,384]{2,1,0:T(8,128)(2,1)S(1)}, u32[]{:S(2)}, u32[]{:S(2)}) collective-permute-start(bf16[1,192,384]{2,1,0:T(8,128)(2,1)S(1)} %slice.562), channel_id=1, source_target_pairs={{0,16},{4,20},{8,24},{12,28},{16,0},{20,4},{24,8},{28,12},{1,17},{... | collective-permute-start | bytes 442376 | tf_op jit(solution)/shard_map/ppermute | solution.py:36
  221.1 7.2 %collective-permute-start.36 = (bf16[192,384]{1,0:T(8,128)(2,1)S(1)}, bf16[192,384]{1,0:T(8,128)(2,1)S(1)}, u32[]{:S(2)}, u32[]{:S(2)}) collective-permute-start(bf16[192,384]{1,0:T(8,128)(2,1)S(1)} %pad_maximum_fusion.10), channel_id=1, source_target_pairs={{0,1},{1,0},{2,3},{3,2},{4,5},{5,4},{6,7},{7,6},{8,9},{9,8},{10,11... | collective-permute-start | bytes 442376 | tf_op jit(solution)/shard_map/ppermute | solution.py:36
  228.5 6.9 %collective-permute-start.37 = (bf16[192,192]{1,0:T(8,128)(2,1)S(1)}, bf16[192,192]{1,0:T(8,128)(2,1)S(1)}, u32[]{:S(2)}, u32[]{:S(2)}) collective-permute-start(bf16[192,192]{1,0:T(8,128)(2,1)S(1)} %fusion.29), channel_id=1, source_target_pairs={{0,2},{1,3},{2,0},{3,1},{4,6},{5,7},{6,4},{7,5},{8,10},{9,11},{10,... | collective-permute-start | bytes 221192 | tf_op jit(solution)/shard_map/ppermute | solution.py:36
  229.7 12.1 %collective-permute-start.43 = (bf16[192,768]{1,0:T(8,128)(2,1)S(1)}, bf16[192,768]{1,0:T(8,128)(2,1)S(1)}, u32[]{:S(2)}, u32[]{:S(2)}) collective-permute-start(bf16[192,768]{1,0:T(8,128)(2,1)S(1)} %pad_maximum_fusion.5), channel_id=1, source_target_pairs={{0,2},{1,3},{2,0},{3,1},{4,6},{5,7},{6,4},{7,5},{8,10},{9,11},{10,... | collective-permute-start | bytes 884744 | tf_op jit(solution)/shard_map/ppermute | solution.py:36
  237.0 29.4 %collective-permute-start.23 = (bf16[2,2,224,768]{3,2,1,0:T(8,128)(2,1)S(1)}, bf16[2,2,224,768]{3,2,1,0:T(8,128)(2,1)S(1)}, u32[]{:S(2)}, u32[]{:S(2)}) collective-permute-start(bf16[2,2,224,768]{3,2,1,0:T(8,128)(2,1)S(1)} %add_convert_fusion), channel_id=1, source_target_pairs={{0,1},{1,0},{2,3},{3,2},{4,5},{5,4},{6,7},{7,6},{8,9},{9,8},{10,11... | collective-permute-start | bytes 4128776 | tf_op jit(solution)/shard_map/ppermute | solution.py:36
  238.2 4.5 %collective-permute-start.38 = (f32[96,192]{1,0:T(8,128)S(1)}, f32[96,192]{1,0:T(8,128)S(1)}, u32[]{:S(2)}, u32[]{:S(2)}) collective-permute-start(f32[96,192]{1,0:T(8,128)S(1)} %slice_select_fusion.8), channel_id=1, source_target_pairs={{0,4},{4,0},{8,12},{12,8},{16,20},{20,16},{24,28},{28,24},{1,5},{5... | collective-permute-start | bytes 221192 | tf_op jit(solution)/shard_map/ppermute | solution.py:36
  242.6 1.8 collective-permute-start.44
  (31 other events, 239.8 us)

commit v2 on v1

--- a/solution.py
+++ b/solution.py
@@ -14,7 +14,7 @@
 TRUNK = 8
 FIRST_LEAF = 10
 TILE = 64
-HEADS_STEP = 4
+HEADS_STEP = 12
 NORM_EPS = 1e-05
 MASKED = -1000000000.0
 BF = jnp.bfloat16
@@ -99,21 +99,11 @@
     return [pieces[r] for r in range(count)]
 
 
-def tp_scatter(pieces, axis):
-    pieces = dict(enumerate(pieces))
-    bits = bits_of(len(pieces))
-    for bit in bits:
-        kept = [r for r in sorted(pieces) if not r & bit]
-        sent = [pieces[r | bit] for r in kept]
-        sent = sent[0] if len(sent) == 1 else jnp.concatenate(sent, axis=axis)
-        taken = swap_tp(sent.astype(BF), bit).astype(F32)
-        size = taken.shape[axis] // len(kept)
-        pieces = {
-            r: pieces[r].astype(F32)
-            + lax.slice_in_dim(taken, place * size, (place + 1) * size, axis=axis)
-            for place, r in enumerate(kept)
-        }
-    return pieces[0]
+def tp_scatter_direct(pieces):
+    total = pieces[0].astype(F32)
+    for r in range(1, len(pieces)):
+        total = total + swap_tp(pieces[r].astype(BF), r).astype(F32)
+    return total
 
 
 def tp_scatter_even(value, size):
@@ -311,11 +301,11 @@
         cost_estimate=pl.CostEstimate(
             flops=2 * 256 * work, bytes_accessed=2 * rows * width, transcendentals=work // 6
         ),
-        compiler_params=pltpu.CompilerParams(vmem_limit_bytes=40 * 2**20),
+        compiler_params=pltpu.CompilerParams(vmem_limit_bytes=36 * 2**20),
     )(meta, query_lin, grad_attended, key_value, cos, back, ahead, *(earlier or ()))
 
 
-def local_kernel(kernel, outs, args, scratch=(), flops=0, scalars=1):
+def local_kernel(kernel, outs, args, scratch=(), flops=0, scalars=1, mib=56):
     return pl.pallas_call(
         kernel,
         out_shape=[jax.ShapeDtypeStruct(shape, kind) for shape, kind in outs],
@@ -324,7 +314,7 @@
         out_specs=[pl.BlockSpec(memory_space=pltpu.VMEM)] * len(outs),
         scratch_shapes=list(scratch),
         cost_estimate=pl.CostEstimate(flops=flops, bytes_accessed=2**20, transcendentals=0),
-        compiler_params=pltpu.CompilerParams(vmem_limit_bytes=56 * 2**20),
+        compiler_params=pltpu.CompilerParams(vmem_limit_bytes=mib * 2**20),
     )(*args)
 
 
@@ -694,6 +684,7 @@
             pltpu.VMEM((4 * rows, hidden_own), BF),
             pltpu.VMEM((width, hidden_own), F32),
         ],
+        mib=56,
         flops=12 * 4 * rows * width * hidden_own,
     )
     part_kept, part_sent, ffn_vectors, up_kept, down_kept = ffn_out[:5]
@@ -711,7 +702,7 @@
 
     attended_out = dot(attended, out_mat, 1, 1)
     kv_pieces = relative(kv_grad.T, 0, "tp").reshape(tp_count, rows, -1)
-    kv_sum = tp_scatter([kv_pieces[r] for r in range(tp_count)], 0)
+    kv_sum = tp_scatter_direct([kv_pieces[r] for r in range(tp_count)])
     kv_low_grad = (
         kv_sum * cos_key
         - jnp.roll(kv_sum, -(ROT // 2), 1) * back_key
@@ -722,11 +713,13 @@
         [((blocks, block_rows, width), BF)] * 2,
         [place, low_one, query_low, cotangent, attended],
         [pltpu.VMEM((width, width), F32)] * 2,
+        mib=56,
         flops=4 * rows * width * width,
     )
     grad_kv_mat = dot(low_one, kv_low_grad, 0, 0)
     norm_one_grad = dot(query_low, query_mat, 1, 1) + dot(kv_low_grad, kv_mat, 1, 1)
-    mat_own = add_low(mat_own, swap_fsdp(mat_given, 1))
+    mat_given = swap_fsdp(mat_given, 1)
+    mat_own = add_low(mat_own, mat_given)
     if blocks > 1:
         side = width // 2
         left = chip_scatter(mat_own[::2, :, :side], mat_own[1::2, :, :side], (2, 4))
@@ -734,8 +727,8 @@
         mat_sum = jnp.concatenate([left, right], axis=1)
     else:
         mat_sum = chip_scatter(mat_own, None, None)
-    mat_sum = tp_scatter(
-        [mat_sum[:, r * heads_tp : (r + 1) * heads_tp] for r in range(tp_count)], 1
+    mat_sum = tp_scatter_direct(
+        [mat_sum[:, r * heads_tp : (r + 1) * heads_tp] for r in range(tp_count)]
     )
     mat_own = pick(mat_sum[:shard], mat_sum[shard:])
     mat_away = swap_fsdp(pick(mat_sum[shard:], mat_sum[:shard]), 1)
@@ -777,8 +770,7 @@
     for bit in reversed(bits_of(fsdp_count)[1:]):
         half = vectors.shape[0] // 2
         vectors = vectors[:half] + swap_fsdp(vectors[half:], bit)
-    for bit in bits_of(tp_count):
-        vectors = vectors + swap_tp(vectors, bit)
+    vectors = vectors + sum(swap_tp(vectors, r) for r in range(1, tp_count))
     output, input_grad = finish(
         *(part_kept, part_core, part_tp, tokens, cotangent, attended_out),
         *(norm_one_grad, gain_one, gain_two, out_shift + down_shift),

time: 274 us -> 270 us (0.985)
  Pallas kernels: 81.8 us -> 69.6 us
  waiting for transfers between devices: 90.4 us -> 99.8 us
  starting transfers between devices: 46.2 us -> 53.3 us
  local copies, waits for them, and re-layouts: 19.7 us -> 14.9 us
    pallas_call x2, Pallas kernels: 44.4 us -> 32.1 us  [attention(): pl.pallas_call(lambda *refs: attention_kernel(first, *refs), out_shape=(j...]
    ppermute x45 -> x48, waiting for transfers between devices: 90.4 us -> 99.8 us  [swap(): return lax.ppermute(value, axis, [(i, i ^ bit) for i in range(count)])]
    ppermute x45 -> x48, starting transfers between devices: 46.2 us -> 53.3 us  [swap(): return lax.ppermute(value, axis, [(i, i ^ bit) for i in range(count)])]
  transfers between devices with their start and end apart: 45 -> 48, of which waited for: 24 -> 21; matrix products, arithmetic and copies ran while one was open for 17% -> 15% of each run, Pallas kernels for 19% -> 15%
where the time goes in v2:
time: 270 us
  waiting for transfers between devices  99.8 us (37%)
  Pallas kernels  69.6 us (26%)
  starting transfers between devices  53.3 us (20%)
  other arithmetic  18.6 us (7%)
  local copies, waits for them, and re-layouts  14.9 us (6%)
  matrix products  12 us (4%)
    ppermute x48, waiting for transfers between devices, swap(): return lax.ppermute(value, axis, [(i, i ^ bit) for i in range(count)])  99.8 us
    ppermute x48, starting transfers between devices, swap(): return lax.ppermute(value, axis, [(i, i ^ bit) for i in range(count)])  53.3 us
    pallas_call x4, Pallas kernels, local_kernel(): pl.pallas_call(kernel, out_shape=[jax.ShapeDtypeStruct(shape, kind) for s...  32.5 us
    pallas_call x2, Pallas kernels, attention(): pl.pallas_call(lambda *refs: attention_kernel(first, *refs), out_shape=(j...  32.1 us
    dot_general x7, matrix products, dot(): lax.dot_general(left, right, (((left_dim,), (right_dim,)), ((), ())), pre...  11.7 us
  transfers between devices with their start and end apart: 48, of which 21 were waited for; matrix products, arithmetic and copies ran while one was open for 15% of the time, Pallas kernels for 15%

profile of v2, /device:TPU:0, one launch (start us, length us, event | category | flops | bytes accessed | tf_op | source)
XLA Modules:
  0.0 269.8 jit_solution(16170794447860281615)
XLA Ops:
  1.3 2.0 shard_map.305
  7.0 1.5 fusion.7
  9.3 2.6 collective-permute-start.1
  11.9 2.5 collective-permute-done.1
  14.4 1.8 collective-permute-start.2
  16.4 2.7 collective-permute-start.6
  24.5 2.8 %collective-permute-start.3 = (bf16[464,128]{1,0:T(8,128)(2,1)S(1)}, bf16[464,128]{1,0:T(8,128)(2,1)S(1)}, u32[]{:S(2)}, u32[]{:S(2)}) collective-permute-start(bf16[464,128]{1,0:T(8,128)(2,1)S(1)} %pad_maximum_fusion.9), channel_id=1, source_target_pairs={{0,2},{1,3},{2,0},{3,1},{4,6},{5,7},{6,4},{7,5},{8,10},{9,11},{10,... | collective-permute-start | bytes 356360 | tf_op jit(solution)/shard_map/ppermute | solution.py:36
  27.4 1.6 collective-permute-start.7
  30.7 1.6 collective-permute-done.3
  33.6 3.0 %collective-permute-start.10 = (bf16[192,768]{1,0:T(8,128)(2,1)S(1)}, bf16[192,768]{1,0:T(8,128)(2,1)S(1)}, u32[]{:S(2)}, u32[]{:S(2)}) collective-permute-start(bf16[192,768]{1,0:T(8,128)(2,1)S(1)} %pad_maximum_fusion.4.refs_0_), channel_id=1, source_target_pairs={{0,24},{4,28},{8,16},{12,20},{16,8},{20,12},{24,0},{28,4},{1,25},{... | collective-permute-start | bytes 884744 | tf_op jit(solution)/shard_map/ppermute | solution.py:36
  37.3 7.2 %collective-permute-done.10.refs_3_ = bf16[192,768]{1,0:T(8,128)(2,1)S(1)} collective-permute-done((bf16[192,768]{1,0:T(8,128)(2,1)S(1)}, bf16[192,768]{1,0:T(8,128)(2,1)S(1)}, u32[]{:S(2)}, u32[]{:S(2)}) %collective-permute-start.10) | collective-permute-done | bytes 294944 | tf_op jit(solution)/shard_map/ppermute | solution.py:36
  44.5 3.6 %collective-permute-done.9.refs_2_ = bf16[192,768]{1,0:T(8,128)(2,1)S(1)} collective-permute-done((bf16[192,768]{1,0:T(8,128)(2,1)S(1)}, bf16[192,768]{1,0:T(8,128)(2,1)S(1)}, u32[]{:S(2)}, u32[]{:S(2)}) %collective-permute-start.9) | collective-permute-done | bytes 294944 | tf_op jit(solution)/shard_map/ppermute | solution.py:36
  50.1 2.3 shard_map.306
  55.0 7.4 %collective-permute-done.18 = bf16[192,768]{1,0:T(8,128)(2,1)} collective-permute-done((bf16[192,768]{1,0:T(8,128)(2,1)S(1)}, bf16[192,768]{1,0:T(8,128)(2,1)}, u32[]{:S(2)}, u32[]{:S(2)}) %collective-permute-start.18) | collective-permute-done | bytes 294944 | tf_op jit(solution)/shard_map/ppermute | solution.py:36
  64.3 2.2 fusion.8.refs_2_
  67.3 22.4 %shard_map.307 = (bf16[448,768]{1,0:T(8,128)(2,1)S(1)}, bf16[448,768]{1,0:T(8,128)(2,1)S(1)}, f32[128,1792]{1,0:T(8,128)S(1)}) custom-call(s32[7,3]{1,0:T(8,128)S(1)} %pad_add_fusion.refs_0_, f32[448,768]{1,0:T(8,128)S(1)} %convolution_add_fusion.1.refs_1_, bf16[448,768]{1,0:T(8,128)(2,1)S(1)} %fusion.8.refs_2_, ...), custom_call_target="tpu_custom_call" | custom-call | flops 15099494400 | bytes 688128 | tf_op jit(solution)/shard_map/pallas_call | solution.py:277
  89.7 9.6 %shard_map.308 = (bf16[448,768]{1,0:T(8,128)(2,1)S(1)}, bf16[448,768]{1,0:T(8,128)(2,1)S(1)}, f32[128,1792]{1,0:T(8,128)S(1)}) custom-call(s32[7,3]{1,0:T(8,128)S(1)} %pad_add_fusion.refs_0_, f32[448,768]{1,0:T(8,128)S(1)} %convolution_add_fusion.1.refs_1_, bf16[448,768]{1,0:T(8,128)(2,1)S(1)} %fusion.8.refs_2_, ...), custom_call_target="tpu_custom_call", output_to_operand_aliasing={{0}: (7, {}), {1}: (8, {})} | custom-call | flops 6039797760 | bytes 688128 | tf_op jit(solution)/shard_map/pallas_call | solution.py:277
  99.7 2.2 collective-permute-start.24
  102.0 2.3 collective-permute-start.26
  106.0 2.3 collective-permute-start.21
  108.3 5.0 %collective-permute-done.25 = bf16[448,128]{1,0:T(8,128)(2,1)S(1)} collective-permute-done((bf16[448,128]{1,0:T(8,128)(2,1)S(1)}, bf16[448,128]{1,0:T(8,128)(2,1)S(1)}, u32[]{:S(2)}, u32[]{:S(2)}) %collective-permute-start.25) | collective-permute-done | bytes 114720 | tf_op jit(solution)/shard_map/ppermute | solution.py:36
  115.4 1.5 fusion.72
  116.9 1.6 collective-permute-start.20
  120.0 3.5 %fusion.6 = (f32[768]{0:T(1024)S(1)}, f32[768]{0:T(1024)S(1)}, f32[448,768]{1,0:T(8,128)}) fusion(bf16[448,768]{1,0:T(8,128)(2,1)} %tokens.1, f32[448]{0:T(512)S(1)} %add_rsqrt_fusion, f32[448]{0:T(512)S(1)} %broadcast_multiply_fusion, f32[448,768]{1,0:T(8,128)} %fusion.72, bf16[448,768]{1,0:T(8,128)(2,1)S(1)} %get-tuple-element.72.query_low, ...), kind=kOutput, calls=%fused_computation.12 | convolution fusion | flops 531479040 | bytes 6497793 | tf_op jit(solution)/shard_map/dot_general | solution.py:25
  124.1 10.9 %collective-permute-done.20.refs_14_ = bf16[192,1536]{1,0:T(8,128)(2,1)} collective-permute-done((bf16[192,1536]{1,0:T(8,128)(2,1)}, bf16[192,1536]{1,0:T(8,128)(2,1)}, u32[]{:S(2)}, u32[]{:S(2)}) %collective-permute-start.20) | collective-permute-done | bytes 589856 | tf_op jit(solution)/shard_map/ppermute | solution.py:36
  135.0 23.2 %shard_map.309 = (bf16[2,4,224,768]{3,2,1,0:T(8,128)(2,1)}, bf16[2,4,224,768]{3,2,1,0:T(8,128)(2,1)}, f32[8,768]{1,0:T(8,128)}, bf16[2,192,768]{2,1,0:T(8,128)(2...) custom-call(s32[2]{0:T(128)} %pad_add_fusion.1.place.refs_0_, ...), custom_call_target="tpu_custom_call" | custom-call | flops 12683575296 | bytes 1048576 | tf_op jit(solution)/shard_map/pallas_call | solution.py:309
  161.2 1.5 collective-permute-done.27
  162.7 1.5 collective-permute-start.28
  165.6 2.4 collective-permute-done.28
  168.0 1.5 collective-permute-start.29
  169.5 4.9 %shard_map.310 = (bf16[4,192,768]{2,1,0:T(8,128)(2,1)}, bf16[4,192,768]{2,1,0:T(8,128)(2,1)}) custom-call(s32[2]{0:T(128)} %pad_add_fusion.1.place.refs_0_, bf16[448,768]{1,0:T(8,128)(2,1)} %copy-done.5, bf16[448,768]{1,0:T(8,128)(2,1)} %copy-done.2, bf16[448,768]{1,0:T(8,128)(2,1)} %grad.3, bf16[448,768]{1,0:T(8,128)(2,1)} %copy-done), custom_call_target="tpu_custom_call" | custom-call | flops 1056964608 | bytes 1048576 | tf_op jit(solution)/shard_map/pallas_call | solution.py:309
  174.7 2.8 %collective-permute-start.31 = (f32[1,110,128]{2,1,0:T(8,128)S(1)}, f32[1,110,128]{2,1,0:T(8,128)S(1)}, u32[]{:S(2)}, u32[]{:S(2)}) collective-permute-start(f32[1,110,128]{2,1,0:T(8,128)S(1)} %slice_add_fusion.1), channel_id=1, source_target_pairs={{0,2},{1,3},{2,0},{3,1},{4,6},{5,7},{6,4},{7,5},{8,10},{9,11},{10,... | collective-permute-start | bytes 168968 | tf_op jit(solution)/shard_map/ppermute | solution.py:36
  178.9 3.1 %fusion.12.base = f32[448,768]{1,0:T(8,128)} fusion(bf16[448,768]{1,0:T(8,128)(2,1)S(1)} %copy-done.1, bf16[768,768]{1,0:T(8,128)(2,1)} %collective-permute-done.11, bf16[768,768]{1,0:T(8,128)(2,1)S(1)} %copy-done.8, pred[]{:T(512)S(6)} %eq.25), kind=kOutput, calls=%fused_computation.34 | convolution fusion | flops 529072128 | bytes 4423681 | tf_op jit(solution)/shard_map/dot_general | solution.py:25
  182.6 1.5 collective-permute-start.44
  186.7 1.5 collective-permute-start.34
  188.7 9.5 %collective-permute-done.42 = bf16[2,192,768]{2,1,0:T(8,128)(2,1)S(1)} collective-permute-done((bf16[2,192,768]{2,1,0:T(8,128)(2,1)S(1)}, bf16[2,192,768]{2,1,0:T(8,128)(2,1)S(1)}, u32[]{:S(2)}, u32[]{:S(2)}) %collective-permute-start.42) | collective-permute-done | bytes 589856 | tf_op jit(solution)/shard_map/ppermute | solution.py:36
  198.4 1.5 collective-permute-start.43
  200.8 3.7 %collective-permute-done.34 = bf16[2,192,384]{2,1,0:T(8,128)(2,1)S(1)} collective-permute-done((bf16[2,192,384]{2,1,0:T(8,128)(2,1)S(1)}, bf16[2,192,384]{2,1,0:T(8,128)(2,1)S(1)}, u32[]{:S(2)}, u32[]{:S(2)}) %collective-permute-start.34) | collective-permute-done | bytes 294944 | tf_op jit(solution)/shard_map/ppermute | solution.py:36
  205.3 1.5 collective-permute-start.38
  206.8 1.5 collective-permute-start.35
  208.3 1.9 collective-permute-done.43
  212.1 2.6 collective-permute-start.40
  216.8 9.8 %collective-permute-done.39 = bf16[192,192]{1,0:T(8,128)(2,1)S(1)} collective-permute-done((bf16[192,192]{1,0:T(8,128)(2,1)S(1)}, bf16[192,192]{1,0:T(8,128)(2,1)S(1)}, u32[]{:S(2)}, u32[]{:S(2)}) %collective-permute-start.39) | collective-permute-done | bytes 73760 | tf_op jit(solution)/shard_map/ppermute | solution.py:36
  226.7 1.7 add_convert_fusion
  228.6 2.7 collective-permute-start.23
  231.4 2.4 collective-permute-done.46
  237.1 26.1 %collective-permute-done.23.from_pair = bf16[2,2,224,768]{3,2,1,0:T(8,128)(2,1)S(1)} collective-permute-done((bf16[2,2,224,768]{3,2,1,0:T(8,128)(2,1)}, bf16[2,2,224,768]{3,2,1,0:T(8,128)(2,1)S(1)}, u32[]{:S(2)}, u32[]{:S(2)}) %collective-permute-start.23) | collective-permute-done | bytes 1376288 | tf_op jit(solution)/shard_map/ppermute | solution.py:36
  264.3 5.0 %finish.1 = (bf16[448,768]{1,0:T(8,128)(2,1)}, bf16[448,768]{1,0:T(8,128)(2,1)}) custom-call(bf16[2,4,224,768]{3,2,1,0:T(8,128)(2,1)} %get-tuple-element.69.kept, bf16[2,4,224,768]{3,2,1,0:T(8,128)(2,1)} %copy-done.4, bf16[2,2,224,768]{3,2,1,0:T(8,128)(2,1)} %copy-done.12, bf16[448,768]{1,0:T(8,128)(2,1)} %tokens.1, bf16[448,768]{1,0:T(8,128)(2,1)} %grad.3, ...), custom_call_target="tpu_custom_call" | custom-call | flops 10321920 | bytes 8257536 | tf_op jit(solution)/shard_map/finish/pallas_call | solution.py:421
  (283 shorter events, 48.2 us)
Async XLA Ops:
  3.3 5.9 %collective-permute-start = (bf16[1,112,128]{2,1,0:T(8,128)(2,1)}, bf16[1,112,128]{2,1,0:T(8,128)(2,1)S(1)}, u32[]{:S(2)}, u32[]{:S(2)}) collective-permute-start(bf16[1,112,128]{2,1,0:T(8,128)(2,1)} %bitcast.118), channel_id=1, source_target_pairs={{0,4},{4,0},{8,12},{12,8},{16,20},{20,16},{24,28},{28,24},{1,5},{5... | collective-permute-start | bytes 86024 | tf_op jit(solution)/shard_map/ppermute | solution.py:36
  3.9 12.4 %collective-permute-start.5 = (bf16[96,960]{1,0:T(8,128)(2,1)}, bf16[96,960]{1,0:T(8,128)(2,1)S(1)}, u32[]{:S(2)}, u32[]{:S(2)}) collective-permute-start(bf16[96,960]{1,0:T(8,128)(2,1)} %get-tuple-element.52), channel_id=1, source_target_pairs={{0,4},{4,0},{8,12},{12,8},{16,20},{20,16},{24,28},{28,24},{1,5},{5... | collective-permute-start | bytes 552968 | tf_op jit(solution)/shard_map/ppermute | solution.py:36
  4.0 113.0 %collective-permute-start.16 = (bf16[448,768]{1,0:T(8,128)(2,1)}, bf16[448,768]{1,0:T(8,128)(2,1)}, u32[]{:S(2)}, u32[]{:S(2)}) collective-permute-start(bf16[448,768]{1,0:T(8,128)(2,1)} %grad.3), channel_id=1, source_target_pairs={{0,4},{4,0},{8,12},{12,8},{16,20},{20,16},{24,28},{28,24},{1,5},{5... | collective-permute-start | bytes 2064392 | tf_op jit(solution)/shard_map/ppermute | solution.py:36
  9.3 5.1 %collective-permute-start.1 = (bf16[2,112,128]{2,1,0:T(8,128)(2,1)S(1)}, bf16[2,112,128]{2,1,0:T(8,128)(2,1)S(1)}, u32[]{:S(2)}, u32[]{:S(2)}) collective-permute-start(bf16[2,112,128]{2,1,0:T(8,128)(2,1)S(1)} %maximum_select_fusion.3), channel_id=1, source_target_pairs={{0,8},{4,12},{8,0},{12,4},{16,24},{20,28},{24,16},{28,20},{1,9},{5... | collective-permute-start | bytes 172040 | tf_op jit(solution)/shard_map/ppermute | solution.py:36
  14.4 5.0 %collective-permute-start.2 = (bf16[4,112,128]{2,1,0:T(8,128)(2,1)S(1)}, bf16[4,112,128]{2,1,0:T(8,128)(2,1)S(1)}, u32[]{:S(2)}, u32[]{:S(2)}) collective-permute-start(bf16[4,112,128]{2,1,0:T(8,128)(2,1)S(1)} %pad_maximum_fusion.10), channel_id=1, source_target_pairs={{0,16},{4,20},{8,24},{12,28},{16,0},{20,4},{24,8},{28,12},{1,17},{... | collective-permute-start | bytes 344072 | tf_op jit(solution)/shard_map/ppermute | solution.py:36
  16.4 10.9 %collective-permute-start.6 = (bf16[192,192]{1,0:T(8,128)(2,1)S(1)}, bf16[192,192]{1,0:T(8,128)(2,1)S(1)}, u32[]{:S(2)}, u32[]{:S(2)}) collective-permute-start(bf16[192,192]{1,0:T(8,128)(2,1)S(1)} %slice.502), channel_id=1, source_target_pairs={{0,2},{1,3},{2,0},{3,1},{4,6},{5,7},{6,4},{7,5},{8,10},{9,11},{10,... | collective-permute-start | bytes 221192 | tf_op jit(solution)/shard_map/ppermute | solution.py:36
  24.5 7.8 %collective-permute-start.3 = (bf16[464,128]{1,0:T(8,128)(2,1)S(1)}, bf16[464,128]{1,0:T(8,128)(2,1)S(1)}, u32[]{:S(2)}, u32[]{:S(2)}) collective-permute-start(bf16[464,128]{1,0:T(8,128)(2,1)S(1)} %pad_maximum_fusion.9), channel_id=1, source_target_pairs={{0,2},{1,3},{2,0},{3,1},{4,6},{5,7},{6,4},{7,5},{8,10},{9,11},{10,... | collective-permute-start | bytes 356360 | tf_op jit(solution)/shard_map/ppermute | solution.py:36
  27.4 5.9 %collective-permute-start.7 = (bf16[192,384]{1,0:T(8,128)(2,1)S(1)}, bf16[192,384]{1,0:T(8,128)(2,1)S(1)}, u32[]{:S(2)}, u32[]{:S(2)}) collective-permute-start(bf16[192,384]{1,0:T(8,128)(2,1)S(1)} %pad_maximum_fusion.8), channel_id=1, source_target_pairs={{0,1},{1,0},{2,3},{3,2},{4,5},{5,4},{6,7},{7,6},{8,9},{9,8},{10,11... | collective-permute-start | bytes 442376 | tf_op jit(solution)/shard_map/ppermute | solution.py:36
  32.3 20.1 %collective-permute-start.4 = (bf16[928,128]{1,0:T(8,128)(2,1)S(1)}, bf16[928,128]{1,0:T(8,128)(2,1)S(1)}, u32[]{:S(2)}, u32[]{:S(2)}) collective-permute-start(bf16[928,128]{1,0:T(8,128)(2,1)S(1)} %pad_maximum_fusion.6), channel_id=1, source_target_pairs={{0,1},{1,0},{2,3},{3,2},{4,5},{5,4},{6,7},{7,6},{8,9},{9,8},{10,11... | collective-permute-start | bytes 712712 | tf_op jit(solution)/shard_map/ppermute | solution.py:36
  33.6 10.9 %collective-permute-start.10 = (bf16[192,768]{1,0:T(8,128)(2,1)S(1)}, bf16[192,768]{1,0:T(8,128)(2,1)S(1)}, u32[]{:S(2)}, u32[]{:S(2)}) collective-permute-start(bf16[192,768]{1,0:T(8,128)(2,1)S(1)} %pad_maximum_fusion.4.refs_0_), channel_id=1, source_target_pairs={{0,24},{4,28},{8,16},{12,20},{16,8},{20,12},{24,0},{28,4},{1,25},{... | collective-permute-start | bytes 884744 | tf_op jit(solution)/shard_map/ppermute | solution.py:36
  36.6 11.6 %collective-permute-start.9 = (bf16[192,768]{1,0:T(8,128)(2,1)S(1)}, bf16[192,768]{1,0:T(8,128)(2,1)S(1)}, u32[]{:S(2)}, u32[]{:S(2)}) collective-permute-start(bf16[192,768]{1,0:T(8,128)(2,1)S(1)} %pad_maximum_fusion.4.refs_0_), channel_id=1, source_target_pairs={{0,16},{4,20},{8,24},{12,28},{16,0},{20,4},{24,8},{28,12},{1,17},{... | collective-permute-start | bytes 884744 | tf_op jit(solution)/shard_map/ppermute | solution.py:36
  36.7 12.6 %collective-permute-start.8 = (bf16[192,768]{1,0:T(8,128)(2,1)S(1)}, bf16[192,768]{1,0:T(8,128)(2,1)S(1)}, u32[]{:S(2)}, u32[]{:S(2)}) collective-permute-start(bf16[192,768]{1,0:T(8,128)(2,1)S(1)} %pad_maximum_fusion.4.refs_0_), channel_id=1, source_target_pairs={{0,8},{4,12},{8,0},{12,4},{16,24},{20,28},{24,16},{28,20},{1,9},{5... | collective-permute-start | bytes 884744 | tf_op jit(solution)/shard_map/ppermute | solution.py:36
  44.5 74.1 %collective-permute-start.14 = (bf16[448,768]{1,0:T(8,128)(2,1)}, bf16[448,768]{1,0:T(8,128)(2,1)}, u32[]{:S(2)}, u32[]{:S(2)}) collective-permute-start(bf16[448,768]{1,0:T(8,128)(2,1)} %tokens.1), channel_id=1, source_target_pairs={{0,4},{4,0},{8,12},{12,8},{16,20},{20,16},{24,28},{28,24},{1,5},{5... | collective-permute-start | bytes 2064392 | tf_op jit(solution)/shard_map/ppermute | solution.py:36
  48.2 14.3 %collective-permute-start.18 = (bf16[192,768]{1,0:T(8,128)(2,1)S(1)}, bf16[192,768]{1,0:T(8,128)(2,1)}, u32[]{:S(2)}, u32[]{:S(2)}) collective-permute-start(bf16[192,768]{1,0:T(8,128)(2,1)S(1)} %slice.509), channel_id=1, source_target_pairs={{0,2},{1,3},{2,0},{3,1},{4,6},{5,7},{6,4},{7,5},{8,10},{9,11},{10,... | collective-permute-start | bytes 884744 | tf_op jit(solution)/shard_map/ppermute | solution.py:36
  49.3 40.3 %collective-permute-start.12 = (bf16[448,768]{1,0:T(8,128)(2,1)}, bf16[448,768]{1,0:T(8,128)(2,1)}, u32[]{:S(2)}, u32[]{:S(2)}) collective-permute-start(bf16[448,768]{1,0:T(8,128)(2,1)} %tokens.1), channel_id=1, source_target_pairs={{0,1},{1,0},{2,3},{3,2},{4,5},{5,4},{6,7},{7,6},{8,9},{9,8},{10,11... | collective-permute-start | bytes 2064392 | tf_op jit(solution)/shard_map/ppermute | solution.py:36
  52.4 11.9 %collective-permute-start.11 = (bf16[768,768]{1,0:T(8,128)(2,1)}, bf16[768,768]{1,0:T(8,128)(2,1)}, u32[]{:S(2)}, u32[]{:S(2)}) collective-permute-start(bf16[768,768]{1,0:T(8,128)(2,1)} %shard_map.306), channel_id=1, source_target_pairs={{0,4},{4,0},{8,12},{12,8},{16,20},{20,16},{24,28},{28,24},{1,5},{5... | collective-permute-start | bytes 3538952 | tf_op jit(solution)/shard_map/ppermute | solution.py:36
  62.4 27.3 %collective-permute-start.13 = (bf16[448,768]{1,0:T(8,128)(2,1)}, bf16[448,768]{1,0:T(8,128)(2,1)S(1)}, u32[]{:S(2)}, u32[]{:S(2)}) collective-permute-start(bf16[448,768]{1,0:T(8,128)(2,1)} %grad.3), channel_id=1, source_target_pairs={{0,1},{1,0},{2,3},{3,2},{4,5},{5,4},{6,7},{7,6},{8,9},{9,8},{10,11... | collective-permute-start | bytes 2064392 | tf_op jit(solution)/shard_map/ppermute | solution.py:36
  99.7 6.2 %collective-permute-start.24 = (bf16[448,128]{1,0:T(8,128)(2,1)S(1)}, bf16[448,128]{1,0:T(8,128)(2,1)S(1)}, u32[]{:S(2)}, u32[]{:S(2)}) collective-permute-start(bf16[448,128]{1,0:T(8,128)(2,1)S(1)} %get-tuple-element.168), channel_id=1, source_target_pairs={{0,1},{1,0},{2,3},{3,2},{4,5},{5,4},{6,7},{7,6},{8,9},{9,8},{10,11... | collective-permute-start | bytes 344072 | tf_op jit(solution)/shard_map/ppermute | solution.py:36
  101.9 11.4 %collective-permute-start.25 = (bf16[448,128]{1,0:T(8,128)(2,1)S(1)}, bf16[448,128]{1,0:T(8,128)(2,1)S(1)}, u32[]{:S(2)}, u32[]{:S(2)}) collective-permute-start(bf16[448,128]{1,0:T(8,128)(2,1)S(1)} %get-tuple-element.169), channel_id=1, source_target_pairs={{0,2},{1,3},{2,0},{3,1},{4,6},{5,7},{6,4},{7,5},{8,10},{9,11},{10,... | collective-permute-start | bytes 344072 | tf_op jit(solution)/shard_map/ppermute | solution.py:36
  102.0 11.2 %collective-permute-start.26 = (bf16[448,128]{1,0:T(8,128)(2,1)S(1)}, bf16[448,128]{1,0:T(8,128)(2,1)S(1)}, u32[]{:S(2)}, u32[]{:S(2)}) collective-permute-start(bf16[448,128]{1,0:T(8,128)(2,1)S(1)} %get-tuple-element.170), channel_id=1, source_target_pairs={{0,3},{1,2},{2,1},{3,0},{4,7},{5,6},{6,5},{7,4},{8,11},{9,10},{10,... | collective-permute-start | bytes 344072 | tf_op jit(solution)/shard_map/ppermute | solution.py:36
  106.0 18.1 %collective-permute-start.21 = (bf16[192,1536]{1,0:T(8,128)(2,1)}, bf16[192,1536]{1,0:T(8,128)(2,1)}, u32[]{:S(2)}, u32[]{:S(2)}) collective-permute-start(bf16[192,1536]{1,0:T(8,128)(2,1)} %pad_maximum_fusion.refs_12_), channel_id=1, source_target_pairs={{0,24},{4,28},{8,16},{12,20},{16,8},{20,12},{24,0},{28,4},{1,25},{... | collective-permute-start | bytes 1769480 | tf_op jit(solution)/shard_map/ppermute | solution.py:36
  113.3 21.7 %collective-permute-start.15 = (bf16[448,768]{1,0:T(8,128)(2,1)}, bf16[448,768]{1,0:T(8,128)(2,1)}, u32[]{:S(2)}, u32[]{:S(2)}) collective-permute-start(bf16[448,768]{1,0:T(8,128)(2,1)} %collective-permute-done.12.refs_5_), channel_id=1, source_target_pairs={{0,4},{4,0},{8,12},{12,8},{16,20},{20,16},{24,28},{28,24},{1,5},{5... | collective-permute-start | bytes 2064392 | tf_op jit(solution)/shard_map/ppermute | solution.py:36
  113.3 21.7 %collective-permute-start.17 = (bf16[448,768]{1,0:T(8,128)(2,1)}, bf16[448,768]{1,0:T(8,128)(2,1)}, u32[]{:S(2)}, u32[]{:S(2)}) collective-permute-start(bf16[448,768]{1,0:T(8,128)(2,1)} %copy-done.28), channel_id=1, source_target_pairs={{0,4},{4,0},{8,12},{12,8},{16,20},{20,16},{24,28},{28,24},{1,5},{5... | collective-permute-start | bytes 2064392 | tf_op jit(solution)/shard_map/ppermute | solution.py:36
  116.9 18.0 %collective-permute-start.20 = (bf16[192,1536]{1,0:T(8,128)(2,1)}, bf16[192,1536]{1,0:T(8,128)(2,1)}, u32[]{:S(2)}, u32[]{:S(2)}) collective-permute-start(bf16[192,1536]{1,0:T(8,128)(2,1)} %pad_maximum_fusion.refs_12_), channel_id=1, source_target_pairs={{0,16},{4,20},{8,24},{12,28},{16,0},{20,4},{24,8},{28,12},{1,17},{... | collective-permute-start | bytes 1769480 | tf_op jit(solution)/shard_map/ppermute | solution.py:36
  118.6 16.4 %collective-permute-start.19 = (bf16[192,1536]{1,0:T(8,128)(2,1)}, bf16[192,1536]{1,0:T(8,128)(2,1)}, u32[]{:S(2)}, u32[]{:S(2)}) collective-permute-start(bf16[192,1536]{1,0:T(8,128)(2,1)} %pad_maximum_fusion.refs_12_), channel_id=1, source_target_pairs={{0,8},{4,12},{8,0},{12,4},{16,24},{20,28},{24,16},{28,20},{1,9},{5... | collective-permute-start | bytes 1769480 | tf_op jit(solution)/shard_map/ppermute | solution.py:36
  161.1 1.6 collective-permute-start.27
  162.7 5.3 %collective-permute-start.28 = (f32[2,110,128]{2,1,0:T(8,128)S(1)}, f32[2,110,128]{2,1,0:T(8,128)S(1)}, u32[]{:S(2)}, u32[]{:S(2)}) collective-permute-start(f32[2,110,128]{2,1,0:T(8,128)S(1)} %slice.536), channel_id=1, source_target_pairs={{0,16},{4,20},{8,24},{12,28},{16,0},{20,4},{24,8},{28,12},{1,17},{... | collective-permute-start | bytes 337928 | tf_op jit(solution)/shard_map/ppermute | solution.py:36
  168.0 6.4 %collective-permute-start.29 = (f32[1,110,128]{2,1,0:T(8,128)S(1)}, f32[1,110,128]{2,1,0:T(8,128)S(1)}, u32[]{:S(2)}, u32[]{:S(2)}) collective-permute-start(f32[1,110,128]{2,1,0:T(8,128)S(1)} %slice.538), channel_id=1, source_target_pairs={{0,8},{4,12},{8,0},{12,4},{16,24},{20,28},{24,16},{28,20},{1,9},{5... | collective-permute-start | bytes 168968 | tf_op jit(solution)/shard_map/ppermute | solution.py:36
  174.4 11.9 %collective-permute-start.33 = (bf16[4,192,768]{2,1,0:T(8,128)(2,1)}, bf16[4,192,768]{2,1,0:T(8,128)(2,1)S(1)}, u32[]{:S(2)}, u32[]{:S(2)}) collective-permute-start(bf16[4,192,768]{2,1,0:T(8,128)(2,1)} %get-tuple-element.78), channel_id=1, source_target_pairs={{0,4},{4,0},{8,12},{12,8},{16,20},{20,16},{24,28},{28,24},{1,5},{5... | collective-permute-start | bytes 3538952 | tf_op jit(solution)/shard_map/ppermute | solution.py:36
  174.4 8.2 %collective-permute-start.32 = (f32[1,110,128]{2,1,0:T(8,128)S(1)}, f32[1,110,128]{2,1,0:T(8,128)S(1)}, u32[]{:S(2)}, u32[]{:S(2)}) collective-permute-start(f32[1,110,128]{2,1,0:T(8,128)S(1)} %slice_add_fusion.1), channel_id=1, source_target_pairs={{0,3},{1,2},{2,1},{3,0},{4,7},{5,6},{6,5},{7,4},{8,11},{9,10},{10,... | collective-permute-start | bytes 168968 | tf_op jit(solution)/shard_map/ppermute | solution.py:36
  174.7 9.3 %collective-permute-start.31 = (f32[1,110,128]{2,1,0:T(8,128)S(1)}, f32[1,110,128]{2,1,0:T(8,128)S(1)}, u32[]{:S(2)}, u32[]{:S(2)}) collective-permute-start(f32[1,110,128]{2,1,0:T(8,128)S(1)} %slice_add_fusion.1), channel_id=1, source_target_pairs={{0,2},{1,3},{2,0},{3,1},{4,6},{5,7},{6,4},{7,5},{8,10},{9,11},{10,... | collective-permute-start | bytes 168968 | tf_op jit(solution)/shard_map/ppermute | solution.py:36
  177.5 6.6 %collective-permute-start.30 = (f32[1,110,128]{2,1,0:T(8,128)S(1)}, f32[1,110,128]{2,1,0:T(8,128)S(1)}, u32[]{:S(2)}, u32[]{:S(2)}) collective-permute-start(f32[1,110,128]{2,1,0:T(8,128)S(1)} %slice_add_fusion.1), channel_id=1, source_target_pairs={{0,1},{1,0},{2,3},{3,2},{4,5},{5,4},{6,7},{7,6},{8,9},{9,8},{10,11... | collective-permute-start | bytes 168968 | tf_op jit(solution)/shard_map/ppermute | solution.py:36
  182.0 16.2 %collective-permute-start.42 = (bf16[2,192,768]{2,1,0:T(8,128)(2,1)S(1)}, bf16[2,192,768]{2,1,0:T(8,128)(2,1)S(1)}, u32[]{:S(2)}, u32[]{:S(2)}) collective-permute-start(bf16[2,192,768]{2,1,0:T(8,128)(2,1)S(1)} %copy-done.30), channel_id=1, source_target_pairs={{0,8},{4,12},{8,0},{12,4},{16,24},{20,28},{24,16},{28,20},{1,9},{5... | collective-permute-start | bytes 1769480 | tf_op jit(solution)/shard_map/ppermute | solution.py:36
  182.6 17.3 %collective-permute-start.44 = (bf16[2,192,768]{2,1,0:T(8,128)(2,1)S(1)}, bf16[2,192,768]{2,1,0:T(8,128)(2,1)S(1)}, u32[]{:S(2)}, u32[]{:S(2)}) collective-permute-start(bf16[2,192,768]{2,1,0:T(8,128)(2,1)S(1)} %copy-done.29), channel_id=1, source_target_pairs={{0,16},{4,20},{8,24},{12,28},{16,0},{20,4},{24,8},{28,12},{1,17},{... | collective-permute-start | bytes 1769480 | tf_op jit(solution)/shard_map/ppermute | solution.py:36
  184.1 42.6 %collective-permute-start.22 = (bf16[2,4,224,768]{3,2,1,0:T(8,128)(2,1)S(1)}, bf16[2,4,224,768]{3,2,1,0:T(8,128)(2,1)S(1)}, u32[]{:S(2)}, u32[]{:S(2)}) collective-permute-start(bf16[2,4,224,768]{3,2,1,0:T(8,128)(2,1)S(1)} %copy-done.27), channel_id=1, source_target_pairs={{0,4},{4,0},{8,12},{12,8},{16,20},{20,16},{24,28},{28,24},{1,5},{5... | collective-permute-start | bytes 8257544 | tf_op jit(solution)/shard_map/ppermute | solution.py:36
  186.7 17.8 %collective-permute-start.34 = (bf16[2,192,384]{2,1,0:T(8,128)(2,1)S(1)}, bf16[2,192,384]{2,1,0:T(8,128)(2,1)S(1)}, u32[]{:S(2)}, u32[]{:S(2)}) collective-permute-start(bf16[2,192,384]{2,1,0:T(8,128)(2,1)S(1)} %get-tuple-element.166), channel_id=1, source_target_pairs={{0,8},{4,12},{8,0},{12,4},{16,24},{20,28},{24,16},{28,20},{1,9},{5... | collective-permute-start | bytes 884744 | tf_op jit(solution)/shard_map/ppermute | solution.py:36
  188.2 16.9 %collective-permute-start.37 = (bf16[2,192,384]{2,1,0:T(8,128)(2,1)S(1)}, bf16[2,192,384]{2,1,0:T(8,128)(2,1)S(1)}, u32[]{:S(2)}, u32[]{:S(2)}) collective-permute-start(bf16[2,192,384]{2,1,0:T(8,128)(2,1)S(1)} %get-tuple-element.167), channel_id=1, source_target_pairs={{0,16},{4,20},{8,24},{12,28},{16,0},{20,4},{24,8},{28,12},{1,17},{... | collective-permute-start | bytes 884744 | tf_op jit(solution)/shard_map/ppermute | solution.py:36
  198.4 11.8 %collective-permute-start.43 = (bf16[1,192,768]{2,1,0:T(8,128)(2,1)S(1)}, bf16[1,192,768]{2,1,0:T(8,128)(2,1)S(1)}, u32[]{:S(2)}, u32[]{:S(2)}) collective-permute-start(bf16[1,192,768]{2,1,0:T(8,128)(2,1)S(1)} %slice.560), channel_id=1, source_target_pairs={{0,16},{4,20},{8,24},{12,28},{16,0},{20,4},{24,8},{28,12},{1,17},{... | collective-permute-start | bytes 884744 | tf_op jit(solution)/shard_map/ppermute | solution.py:36
  200.1 10.2 %collective-permute-start.45 = (bf16[1,192,768]{2,1,0:T(8,128)(2,1)S(1)}, bf16[1,192,768]{2,1,0:T(8,128)(2,1)S(1)}, u32[]{:S(2)}, u32[]{:S(2)}) collective-permute-start(bf16[1,192,768]{2,1,0:T(8,128)(2,1)S(1)} %slice.564), channel_id=1, source_target_pairs={{0,8},{4,12},{8,0},{12,4},{16,24},{20,28},{24,16},{28,20},{1,9},{5... | collective-permute-start | bytes 884744 | tf_op jit(solution)/shard_map/ppermute | solution.py:36
  205.3 6.1 %collective-permute-start.38 = (bf16[1,192,384]{2,1,0:T(8,128)(2,1)S(1)}, bf16[1,192,384]{2,1,0:T(8,128)(2,1)S(1)}, u32[]{:S(2)}, u32[]{:S(2)}) collective-permute-start(bf16[1,192,384]{2,1,0:T(8,128)(2,1)S(1)} %slice.550), channel_id=1, source_target_pairs={{0,8},{4,12},{8,0},{12,4},{16,24},{20,28},{24,16},{28,20},{1,9},{5... | collective-permute-start | bytes 442376 | tf_op jit(solution)/shard_map/ppermute | solution.py:36
  206.8 7.8 %collective-permute-start.35 = (bf16[1,192,384]{2,1,0:T(8,128)(2,1)S(1)}, bf16[1,192,384]{2,1,0:T(8,128)(2,1)S(1)}, u32[]{:S(2)}, u32[]{:S(2)}) collective-permute-start(bf16[1,192,384]{2,1,0:T(8,128)(2,1)S(1)} %slice.544), channel_id=1, source_target_pairs={{0,16},{4,20},{8,24},{12,28},{16,0},{20,4},{24,8},{28,12},{1,17},{... | collective-permute-start | bytes 442376 | tf_op jit(solution)/shard_map/ppermute | solution.py:36
  211.5 15.1 %collective-permute-start.39 = (bf16[192,192]{1,0:T(8,128)(2,1)S(1)}, bf16[192,192]{1,0:T(8,128)(2,1)S(1)}, u32[]{:S(2)}, u32[]{:S(2)}) collective-permute-start(bf16[192,192]{1,0:T(8,128)(2,1)S(1)} %get-tuple-element.209), channel_id=1, source_target_pairs={{0,2},{1,3},{2,0},{3,1},{4,6},{5,7},{6,4},{7,5},{8,10},{9,11},{10,... | collective-permute-start | bytes 221192 | tf_op jit(solution)/shard_map/ppermute | solution.py:36
  212.1 14.5 %collective-permute-start.40 = (bf16[192,192]{1,0:T(8,128)(2,1)S(1)}, bf16[192,192]{1,0:T(8,128)(2,1)S(1)}, u32[]{:S(2)}, u32[]{:S(2)}) collective-permute-start(bf16[192,192]{1,0:T(8,128)(2,1)S(1)} %get-tuple-element.210), channel_id=1, source_target_pairs={{0,3},{1,2},{2,1},{3,0},{4,7},{5,6},{6,5},{7,4},{8,11},{9,10},{10,... | collective-permute-start | bytes 221192 | tf_op jit(solution)/shard_map/ppermute | solution.py:36
  214.8 11.8 %collective-permute-start.36 = (bf16[192,192]{1,0:T(8,128)(2,1)S(1)}, bf16[192,192]{1,0:T(8,128)(2,1)S(1)}, u32[]{:S(2)}, u32[]{:S(2)}) collective-permute-start(bf16[192,192]{1,0:T(8,128)(2,1)S(1)} %slice.546), channel_id=1, source_target_pairs={{0,1},{1,0},{2,3},{3,2},{4,5},{5,4},{6,7},{7,6},{8,9},{9,8},{10,11... | collective-permute-start | bytes 221192 | tf_op jit(solution)/shard_map/ppermute | solution.py:36
  215.3 18.5 %collective-permute-start.46 = (bf16[192,768]{1,0:T(8,128)(2,1)S(1)}, bf16[192,768]{1,0:T(8,128)(2,1)S(1)}, u32[]{:S(2)}, u32[]{:S(2)}) collective-permute-start(bf16[192,768]{1,0:T(8,128)(2,1)S(1)} %pad_maximum_fusion.5), channel_id=1, source_target_pairs={{0,2},{1,3},{2,0},{3,1},{4,6},{5,7},{6,4},{7,5},{8,10},{9,11},{10,... | collective-permute-start | bytes 884744 | tf_op jit(solution)/shard_map/ppermute | solution.py:36
  228.6 34.6 %collective-permute-start.23 = (bf16[2,2,224,768]{3,2,1,0:T(8,128)(2,1)}, bf16[2,2,224,768]{3,2,1,0:T(8,128)(2,1)S(1)}, u32[]{:S(2)}, u32[]{:S(2)}) collective-permute-start(bf16[2,2,224,768]{3,2,1,0:T(8,128)(2,1)} %add_convert_fusion), channel_id=1, source_target_pairs={{0,1},{1,0},{2,3},{3,2},{4,5},{5,4},{6,7},{7,6},{8,9},{9,8},{10,11... | collective-permute-start | bytes 4128776 | tf_op jit(solution)/shard_map/ppermute | solution.py:36
  231.3 2.7 %collective-permute-start.41 = (f32[96,192]{1,0:T(8,128)S(1)}, f32[96,192]{1,0:T(8,128)S(1)}, u32[]{:S(2)}, u32[]{:S(2)}) collective-permute-start(f32[96,192]{1,0:T(8,128)S(1)} %slice_select_fusion.8), channel_id=1, source_target_pairs={{0,4},{4,0},{8,12},{12,8},{16,20},{20,16},{24,28},{28,24},{1,5},{5... | collective-permute-start | bytes 221192 | tf_op jit(solution)/shard_map/ppermute | solution.py:36
  233.9 1.6 collective-permute-start.47
  (33 other events, 418.6 us)
